TPU v7x, 256 devices: a whole 4x4x8 slice. The times are simulated.
256 devices in a mesh: blk: 32 (over x, z_lo, core), uly: 8 (over y, z_hi).
Axes of the slice: x: 4, y: 4, z: 8 (z_hi: 2, z_lo: 4; z = z_hi * 4 + z_lo), core: 2. Of those that a mesh axis runs over, the one named last changes fastest.
Arguments:
- video_tokens: bfloat16 [12288, 3072], P(('blk', 'uly')), may hold values from -6 to 6
- text_tokens: bfloat16 [256, 3072], P('uly'), may hold values from -6 to 6
- video_modulation: bfloat16 [3, 3072], replicated, may hold values from -4 to 4
- text_modulation: bfloat16 [3, 3072], replicated, may hold values from -4 to 4
- video_projection: bfloat16 [3072, 3, 2048], P(None, None, 'uly'), may hold values from -0.109375 to 0.109375
- text_projection: bfloat16 [3072, 3, 2048], P(None, None, 'uly'), may hold values from -0.109375 to 0.109375
- video_output: bfloat16 [2048, 3072], P('uly'), may hold values from -0.125 to 0.125
- text_output: bfloat16 [2048, 3072], P('uly'), may hold values from -0.125 to 0.125
- video_gains: float32 [2, 128], replicated, may hold values from 1 to 12
- text_gains: float32 [2, 128], replicated, may hold values from 1 to 12
Outputs:
- video_attention: bfloat16 [12288, 3072], P(('blk', 'uly'))
- text_attention: bfloat16 [256, 3072], P('uly')
All inputs are finite; a program needn't handle non-finite values.
Results may differ from a plain program's by a relative error of at most 0.025.
The roundings to bfloat16 on the way count: a program that leaves them out, or rounds other values in their place, can miss the bound.
Values may be sent and summed in bfloat16 or wider, within the bound.
A program may use at most 128 MiB of HBM per device.

v0:
```python
import jax
import jax.numpy as jnp
from jax import lax
from jax.sharding import Mesh
from jax.sharding import PartitionSpec as P

HD = 128
BLK = ("blk_0", "blk_1", "blk_2")
ULY = ("uly_0", "uly_1")
BLK_ULY = ("blk_0", "blk_1", "blk_2", "uly_0", "uly_1")


EPS_NORM = 1e-06


def collected_together(x, axis):
    leaves = jax.tree.leaves(x)
    turns = sorted(range(len(leaves)), key=lambda k: -leaves[k].size)
    width = (1, *leaves[turns[0]].shape)[-1]
    lines = [
        jnp.pad(leaves[k].reshape(-1), (0, -leaves[k].size % width)).reshape(-1, width)
        for k in turns
    ]
    both, at, found = (lax.all_gather(jnp.concatenate(lines), axis), 0, {})
    for k, line in zip(turns, lines):
        slab = both[:, at : at + len(line)].reshape(len(both), -1)
        found[k] = slab[:, : leaves[k].size].reshape(-1, *leaves[k].shape)
        at += len(line)
    numbers = iter(range(len(leaves)))
    return jax.tree.map(lambda _: found[next(numbers)], x)


def merged_by_axis(x, axes, combine):
    for axis in axes:
        pieces = collected_together(
            jax.tree.map(
                lambda part, kind: part.astype(kind),
                x,
                jax.tree.map(lambda a: jnp.bfloat16 if a.dtype == jnp.float32 else a.dtype, x),
            ),
            axis,
        )
        widened = [
            jax.tree.map(lambda part, own: part[k].astype(own.dtype), pieces, x)
            for k in range(lax.axis_size(axis))
        ]
        x = widened[0]
        for partner_block in widened[1:]:
            x = combine(x, partner_block)
    return x


def summed_rows(terms, axes):
    subtotal = terms.astype(jnp.bfloat16)
    for axis in axes:
        subtotal = lax.psum_scatter(subtotal, axis, scatter_dimension=0, tiled=True)
    return subtotal.astype(jnp.float32)


def split_up(x, dim, length):
    before, after = (x.shape[:dim], x.shape[dim + 1 :])
    return jnp.moveaxis(x.reshape(*before, length, -1, *after), dim, 0)


def summed_on_arrival(x, axis, dim):
    length = lax.axis_size(axis)
    tiles = lax.all_to_all(split_up(x, dim, length), axis, 0, 0, tiled=True)
    return jnp.sum(tiles.astype(jnp.float32), axis=0)


def modulate(rows, factors):
    floats = rows.astype(jnp.float32)
    centre = floats - jnp.mean(floats, axis=-1, keepdims=True)
    spread = jnp.mean(centre * centre, axis=-1, keepdims=True)
    normed = centre / jnp.sqrt(spread + EPS_NORM)
    wide = factors.astype(jnp.float32)
    return (normed * (1.0 + wide[1]) + wide[0]).astype(jnp.bfloat16)


def head_norm(vectors, channel_gain):
    inverse = lax.rsqrt(jnp.mean(vectors * vectors, axis=-1, keepdims=True) + EPS_NORM)
    return (vectors * inverse * channel_gain).astype(jnp.bfloat16)


def project_rows(modded, weights, gains):
    mixture = jnp.einsum("td,dch->tch", modded, weights, preferred_element_type=jnp.float32)
    row_count, col_count = (mixture.shape[0], mixture.shape[2])
    per_head = mixture.reshape(row_count, 3, col_count // HD, HD)
    query_rows = head_norm(per_head[:, 0], gains[0]).reshape(row_count, col_count)
    key_rows = head_norm(per_head[:, 1], gains[1]).reshape(row_count, col_count)
    value_rows = per_head[:, 2].astype(jnp.bfloat16).reshape(row_count, col_count)
    return jnp.stack([query_rows, key_rows, value_rows], axis=1)


def block_scores(query_rows, key_rows):
    heads_here = query_rows.shape[1] // HD
    return jnp.einsum(
        "qhd,khd->hqk",
        query_rows.reshape(-1, heads_here, HD),
        key_rows.reshape(-1, heads_here, HD),
        preferred_element_type=jnp.float32,
    ) * HD ** (-0.5)


def weighted(weights, value_rows):
    heads_here = weights.shape[0]
    return jnp.einsum(
        "hqk,khd->hqd",
        weights.astype(jnp.bfloat16),
        value_rows.reshape(-1, heads_here, HD),
        preferred_element_type=jnp.float32,
    )


def opening(query_rows, key_rows, value_rows):
    scores = block_scores(query_rows, key_rows)
    highest = jnp.max(scores, axis=-1)
    weights = jnp.exp(scores - highest[..., None])
    return (highest, jnp.sum(weights, axis=-1), weighted(weights, value_rows))


def absorb(softmax_state, query_rows, key_rows, value_rows):
    highest, totals, weighted_sums = softmax_state
    scores = block_scores(query_rows, key_rows)
    raised = jnp.maximum(highest, jnp.max(scores, axis=-1))
    shrink = jnp.exp(highest - raised)
    weights = jnp.exp(scores - raised[..., None])
    return (
        raised,
        totals * shrink + jnp.sum(weights, axis=-1),
        weighted_sums * shrink[..., None] + weighted(weights, value_rows),
    )


def combine_states(earlier_state, later_state):
    raised = jnp.maximum(earlier_state[0], later_state[0])
    left_scale = jnp.exp(earlier_state[0] - raised)
    right_scale = jnp.exp(later_state[0] - raised)
    totals = earlier_state[1] * left_scale + later_state[1] * right_scale
    weighted_sums = (
        earlier_state[2] * left_scale[..., None] + later_state[2] * right_scale[..., None]
    )
    return (raised, totals, weighted_sums)


def finalize(softmax_state):
    result = softmax_state[2] / softmax_state[1][..., None]
    return jnp.transpose(result, (1, 0, 2)).reshape(result.shape[1], -1).astype(jnp.bfloat16)


def joint_attention(softmax_state, query_rows, pairs):
    shard_rows = pairs.shape[0]
    piece_rows = lax.all_gather(pairs, BLK, axis=0, tiled=True)
    turn_count = piece_rows.shape[0] // shard_rows
    turn_rows = piece_rows.shape[0] // turn_count

    def one_turn(turn_index, inner_state):
        sliced = lax.dynamic_slice_in_dim(piece_rows, turn_index * turn_rows, turn_rows, 0)
        return absorb(inner_state, query_rows, sliced[:, 0], sliced[:, 1])

    return lax.fori_loop(0, turn_count, one_turn, softmax_state)


def local(
    video_tokens,
    text_tokens,
    video_modulation,
    text_modulation,
    video_projection,
    text_projection,
    video_output,
    text_output,
    video_gains,
    text_gains,
):
    video_proj = project_rows(
        lax.all_gather(modulate(video_tokens, video_modulation), ULY, axis=0, tiled=True),
        video_projection,
        video_gains,
    )
    text_proj = project_rows(
        lax.all_gather(modulate(text_tokens, text_modulation), ULY, axis=0, tiled=True),
        text_projection,
        text_gains,
    )
    video_pairs = video_proj[:, 1:]
    video_state = opening(video_proj[:, 0], text_proj[:, 1], text_proj[:, 2])
    video_heads = finalize(joint_attention(video_state, video_proj[:, 0], video_pairs))
    text_state = opening(text_proj[:, 0], video_proj[:, 1], video_proj[:, 2])
    text_state = merged_by_axis(text_state, BLK, combine_states)
    text_heads = finalize(absorb(text_state, text_proj[:, 0], text_proj[:, 1], text_proj[:, 2]))
    video_summed = summed_rows(
        jnp.dot(video_heads, video_output, preferred_element_type=jnp.float32), ULY
    )
    text_summed = summed_on_arrival(
        jnp.dot(text_heads, text_output, preferred_element_type=jnp.float32).astype(jnp.bfloat16),
        ULY,
        0,
    )
    video_attention = (video_summed * video_modulation[2].astype(jnp.float32)).astype(jnp.bfloat16)
    text_attention = (text_summed * text_modulation[2].astype(jnp.float32)).astype(jnp.bfloat16)
    return (video_attention, text_attention)


def solution(mesh):
    torus = Mesh(mesh.devices.reshape(4, 4, 2, 4, 2), ("blk_0", "blk_1", "blk_2", "uly_0", "uly_1"))
    placed = (
        P(BLK_ULY, None),
        P(ULY, None),
        P(),
        P(),
        P(None, None, ULY),
        P(None, None, ULY),
        P(ULY, None),
        P(ULY, None),
        P(),
        P(),
    )
    return jax.shard_map(
        local,
        mesh=torus,
        in_specs=placed,
        out_specs=(P(BLK_ULY, None), P(ULY, None)),
        check_vma=False,
    )
```

profile of v0, /device:TPU:1, one launch (start us, length us, event | category | flops | bytes accessed | tf_op | source)
XLA Modules:
  0.0 409.4 jit_solution(2178064178969076653)
XLA Ops:
  7.3 0.9 slice.269
  8.1 0.7 convert_element_type.565
  8.9 1.1 convert_reduce_fusion.1
  10.0 1.2 fusion.17
  11.2 1.9 fusion.20
  13.7 0.8 fusion.28
  14.6 81.0 %all-gather.7.cloned.1.call-done = bf16[384,3072]{1,0:T(8,128)(2,1)} async-done(((bf16[48,3072]{1,0:T(8,128)(2,1)}), bf16[384,3072]{1,0:T(8,128)(2,1)}) %all-gather.7.cloned.1.call-update) | async-done | bytes 2359312 | tf_op jit(solution)/shard_map/all_gather | solution.py:177
  95.6 5.3 %fusion.5 = f32[384,3,256]{0,2,1:T(8,128)S(1)} fusion(bf16[3072,3,256]{2,0,1:T(8,128)(2,1)} %param.16, bf16[384,3072]{1,0:T(8,128)(2,1)} %all-gather.7.cloned.1.call-done), kind=kOutput, calls=%fused_computation.14 | convolution fusion | flops 1811939328 | bytes 8257536 | tf_op jit(solution)/shard_map/td,dch->tch/dot_general | solution.py:86
  101.1 0.8 copy.39
  101.9 0.8 fusion.152
  103.7 0.8 pad_maximum_fusion
  104.5 56.8 %all-gather.9.cloned.1.call-done = bf16[256,3072]{1,0:T(8,128)(2,1)} async-done(((bf16[32,3072]{1,0:T(8,128)(2,1)}), bf16[256,3072]{1,0:T(8,128)(2,1)}) %all-gather.9.cloned.1.call-update) | async-done | bytes 1572880 | tf_op jit(solution)/shard_map/all_gather | solution.py:182
  161.3 5.6 %fusion.7 = f32[256,3,256]{0,2,1:T(8,128)} fusion(bf16[3072,3,256]{2,0,1:T(8,128)(2,1)} %param.17, bf16[256,3072]{1,0:T(8,128)(2,1)} %all-gather.9.cloned.1.call-done), kind=kOutput, calls=%fused_computation.16 | convolution fusion | flops 1207959552 | bytes 7077888 | tf_op jit(solution)/shard_map/td,dch->tch/dot_general | solution.py:86
  166.9 1.0 slice.274
  167.9 0.8 copy.59
  168.7 1.1 fusion.153
  170.3 1.2 fusion.156
  171.5 1.0 copy.54
  173.6 12.1 %all-gather = bf16[2080,128]{1,0:T(8,128)(2,1)S(1)} all-gather(bf16[520,128]{1,0:T(8,128)(2,1)S(1)} %pad_maximum_fusion.1), channel_id=2, replica_groups=mesh['blk_0'=4,'blk_1'=4,'blk_2'=2,'uly_0'=4,'uly_1'=2] {'blk_0'}, dimensions={0}, use_global_device_ids=true | all-gather | bytes 665600 | tf_op jit(solution)/shard_map/all_gather | solution.py:24
  187.5 59.0 %all-gather.11.cloned.1.call-done = bf16[12288,2,256]{0,2,1:T(8,128)(2,1)} async-done(((bf16[384,2,256]{0,2,1:T(8,128)(2,1)}), bf16[12288,2,256]{0,2,1:T(8,128)(2,1)}) %all-gather.11.cloned.1.call-update) | async-done | bytes 12582928 | tf_op jit(solution)/shard_map/all_gather | solution.py:153
  246.5 71.0 %while.17 = (s32[]{:T(128)}, f32[2,384]{1,0:T(2,128)S(1)}, f32[2,384]{1,0:T(2,128)S(1)}, f32[2,384,128]{2,1,0:T(8,128)S(1)}, bf16[12288,2,256]{0,2,1:T(8,128)(2,...) while((s32[]{:T(128)}, f32[2,384]{1,0:T(2,128)S(1)}, ...), condition=%wide.region_12.13_spmd, body=%wide.region_9.12_spmd.sunk | while | flops 152962560 | bytes 5750959 | solution.py:161
  246.5 1.1 constant_dynamic-slice_fusion.3
  248.7 1.1 constant_dynamic-slice_fusion.3
  250.9 1.1 constant_dynamic-slice_fusion.3
  253.2 1.1 constant_dynamic-slice_fusion.3
  255.4 1.1 constant_dynamic-slice_fusion.3
  257.6 1.1 constant_dynamic-slice_fusion.3
  259.8 1.1 constant_dynamic-slice_fusion.3
  262.0 1.1 constant_dynamic-slice_fusion.3
  264.3 1.1 constant_dynamic-slice_fusion.3
  266.5 1.1 constant_dynamic-slice_fusion.3
  268.7 1.1 constant_dynamic-slice_fusion.3
  270.9 1.1 constant_dynamic-slice_fusion.3
  273.1 1.1 constant_dynamic-slice_fusion.3
  275.4 1.1 constant_dynamic-slice_fusion.3
  277.6 1.1 constant_dynamic-slice_fusion.3
  279.8 1.1 constant_dynamic-slice_fusion.3
  282.0 1.1 constant_dynamic-slice_fusion.3
  284.2 1.1 constant_dynamic-slice_fusion.3
  286.5 1.1 constant_dynamic-slice_fusion.3
  288.7 1.1 constant_dynamic-slice_fusion.3
  290.9 1.1 constant_dynamic-slice_fusion.3
  293.1 1.1 constant_dynamic-slice_fusion.3
  295.3 1.1 constant_dynamic-slice_fusion.3
  297.6 1.1 constant_dynamic-slice_fusion.3
  299.8 1.1 constant_dynamic-slice_fusion.3
  302.0 1.1 constant_dynamic-slice_fusion.3
  304.2 1.1 constant_dynamic-slice_fusion.3
  306.4 1.1 constant_dynamic-slice_fusion.3
  308.7 1.1 constant_dynamic-slice_fusion.3
  310.9 1.1 constant_dynamic-slice_fusion.3
  313.1 1.1 constant_dynamic-slice_fusion.3
  315.3 1.1 constant_dynamic-slice_fusion.3
  317.7 2.2 convolution_convert_fusion
  320.0 13.4 %all-gather.1 = bf16[2080,128]{1,0:T(8,128)(2,1)S(1)} all-gather(bf16[520,128]{1,0:T(8,128)(2,1)S(1)} %pad_maximum_fusion.2), channel_id=3, replica_groups=mesh['blk_0'=4,'blk_1'=4,'blk_2'=2,'uly_0'=4,'uly_1'=2] {'blk_1'}, dimensions={0}, use_global_device_ids=true | all-gather | bytes 665600 | tf_op jit(solution)/shard_map/all_gather | solution.py:24
  334.0 4.5 %all-gather.2 = bf16[1040,128]{1,0:T(8,128)(2,1)S(1)} all-gather(bf16[520,128]{1,0:T(8,128)(2,1)S(1)} %pad_maximum_fusion.3), channel_id=4, replica_groups=mesh['blk_0'=4,'blk_1'=4,'blk_2'=2,'uly_0'=4,'uly_1'=2] {'blk_2'}, dimensions={0}, use_global_device_ids=true | all-gather | bytes 399360 | tf_op jit(solution)/shard_map/all_gather | solution.py:24
  339.2 1.0 copy-done.4
  340.2 1.8 convolution_convert_fusion.1
  342.0 6.5 %all-to-all-start = ((bf16[8,32,3072]{2,1,0:T(8,128)(2,1)}), bf16[8,32,3072]{2,1,0:T(8,128)(2,1)S(1)}, u32[]{:S(2)}, u32[]{:S(2)}) async-start(bf16[8,32,3072]{2,1,0:T(8,128)(2,1)} %bitcast.68), calls=%async_computation.2 | async-start | bytes 3145728 | tf_op jit(solution)/shard_map/all_to_all | solution.py:67
  348.5 3.9 reduce-scatter.3.cloned.1.call-done
  352.5 33.4 %all-to-all-done = bf16[8,32,3072]{2,1,0:T(8,128)(2,1)S(1)} async-done(((bf16[8,32,3072]{2,1,0:T(8,128)(2,1)}), bf16[8,32,3072]{2,1,0:T(8,128)(2,1)S(1)}, u32[]{:S(2)}, u32[]{:S(2)}) %all-to-all-start) | async-done | bytes 1572896 | tf_op jit(solution)/shard_map/all_to_all | solution.py:67
  386.1 0.7 multiply_convert_fusion.1
  386.8 14.3 %reduce-scatter.5.cloned.1.call-done = bf16[48,3072]{1,0:T(8,128)(2,1)} async-done(((bf16[96,3072]{1,0:T(8,128)(2,1)}), bf16[48,3072]{1,0:T(8,128)(2,1)}) %reduce-scatter.5.cloned.1.call-update) | async-done | bytes 294928 | tf_op jit(solution)/shard_map/reduce_scatter | solution.py:56
  401.1 1.7 multiply_convert_fusion
  (287 shorter events, 42.1 us)
Async XLA Ops:
  7.2 310.6 %copy-start = (bf16[256,3072]{1,0:T(8,128)(2,1)S(1)}, bf16[256,3072]{1,0:T(8,128)(2,1)}, u32[]{:S(2)}) copy-start(bf16[256,3072]{1,0:T(8,128)(2,1)} %param.18) | copy-start | bytes 4718596
  7.2 6.0 %copy-start.9 = (bf16[3,3072]{1,0:T(4,128)(2,1)S(1)}, bf16[3,3072]{1,0:T(4,128)(2,1)}, u32[]{:S(2)}) copy-start(bf16[3,3072]{1,0:T(4,128)(2,1)} %param.15) | copy-start | bytes 55300
  7.2 6.0 %copy-start.3 = (bf16[32,3072]{1,0:T(8,128)(2,1)S(1)}, bf16[32,3072]{1,0:T(8,128)(2,1)}, u32[]{:S(2)}) copy-start(bf16[32,3072]{1,0:T(8,128)(2,1)} %param.13) | copy-start | bytes 589828
  7.2 7.4 %copy-start.10 = (f32[2,128]{1,0:T(2,128)S(1)}, f32[2,128]{1,0:T(2,128)}, u32[]{:S(2)}) copy-start(f32[2,128]{1,0:T(2,128)} %param.21) | copy-start | bytes 3076
  7.2 7.4 %copy-start.11 = (f32[2,128]{1,0:T(2,128)S(1)}, f32[2,128]{1,0:T(2,128)}, u32[]{:S(2)}) copy-start(f32[2,128]{1,0:T(2,128)} %param.20) | copy-start | bytes 3076
  7.2 88.4 %all-gather.7.cloned.1.call-start = ((), (), s32[]{:S(2)}) async-start(), calls=%async_computation.3 | async-start | bytes 2654208 | tf_op jit(solution)/shard_map/all_gather | solution.py:177
  13.1 148.2 %all-gather.9.cloned.1.call-start = ((), (), s32[]{:S(2)}) async-start(), calls=%async_computation.4 | async-start | bytes 1769472 | tf_op jit(solution)/shard_map/all_gather | solution.py:182
  14.5 232.0 %all-gather.11.cloned.1.call-start = ((), (), s32[]{:S(2)}) async-start(), calls=%async_computation.5 | async-start | bytes 12976128 | tf_op jit(solution)/shard_map/all_gather | solution.py:153
  102.7 0.9 copy-start.6
  104.5 247.9 %reduce-scatter.3.cloned.1.call-start = ((), (), s32[]{:S(2)}) async-start(), calls=%async_computation.6 | async-start | bytes 2949120 | tf_op jit(solution)/shard_map/reduce_scatter | solution.py:56
  169.7 1.8 copy-start.5
  173.3 13.0 %copy-start.1 = (f32[384,1,2,128]{3,0,2,1:T(8,128)S(1)}, f32[384,1,2,128]{3,0,2,1:T(8,128)}, u32[]{:S(2)}) copy-start(f32[384,1,2,128]{3,0,2,1:T(8,128)} %copy.54) | copy-start | bytes 1179652
  186.3 0.9 copy-start.7
  320.0 18.8 %copy-start.2 = (f32[2,256,256]{1,2,0:T(8,128)S(1)}, f32[2,256,256]{1,2,0:T(8,128)}, u32[]{:S(2)}) copy-start(f32[2,256,256]{1,2,0:T(8,128)} %get-tuple-element.171) | copy-start | bytes 1572868
  338.8 1.4 copy-start.4
  342.0 6.5 %copy-start.8 = (bf16[3,3072]{1,0:T(4,128)(2,1)S(1)}, bf16[3,3072]{1,0:T(4,128)(2,1)}, u32[]{:S(2)}) copy-start(bf16[3,3072]{1,0:T(4,128)(2,1)} %param.14) | copy-start | bytes 55300
  342.0 43.9 %all-to-all-start = ((bf16[8,32,3072]{2,1,0:T(8,128)(2,1)}), bf16[8,32,3072]{2,1,0:T(8,128)(2,1)S(1)}, u32[]{:S(2)}, u32[]{:S(2)}) async-start(bf16[8,32,3072]{2,1,0:T(8,128)(2,1)} %bitcast.68), calls=%async_computation.2 | async-start | bytes 3145728 | tf_op jit(solution)/shard_map/all_to_all | solution.py:67
  348.4 52.7 %reduce-scatter.5.cloned.1.call-start = ((), (), s32[]{:S(2)}) async-start(), calls=%async_computation.7 | async-start | bytes 884736 | tf_op jit(solution)/shard_map/reduce_scatter | solution.py:56
Sparse Core Ops, SparseCore 0:
  13.2 82.3 all-gather.6
  98.8 62.4 all-gather.8
  163.1 83.3 all-gather.10
  320.1 32.2 reduce-scatter.2
  354.8 46.3 reduce-scatter.4
where the time goes:
time: 412 us; the launch traced here: 409 us
  waiting for transfers between devices  249 us (60%)
  matrix products  46.4 us (11%)
  local copies, waits for them, and re-layouts  43.2 us (10%)
  blocking collectives  30 us (7%)
  other arithmetic  18.7 us (5%)
  between operations  14.3 us (3%)
  starting transfers between devices  6.67 us (2%)
    all_gather x1, waiting for transfers between devices, local(): lax.all_gather(modulate(video_tokens, video_modulation), ULY, axis=0, til...  81 us
    all_gather x1, waiting for transfers between devices, joint_attention(): piece_rows = lax.all_gather(pairs, BLK, axis=0, tiled=True)  59 us
    all_gather x1, waiting for transfers between devices, local(): lax.all_gather(modulate(text_tokens, text_modulation), ULY, axis=0, tiled...  56.8 us
    slice x32, local copies, waits for them, and re-layouts, one_turn(): return absorb(inner_state, query_rows, sliced[:, 0], sliced[:, 1])  34.2 us
    all_to_all x1, waiting for transfers between devices, summed_on_arrival(): tiles = lax.all_to_all(split_up(x, dim, length), axis, 0, 0, tiled=True)  33.4 us
    all_gather x3, blocking collectives, collected_together(): both, at, found = (lax.all_gather(jnp.concatenate(lines), axis), 0, {})  30 us
    reduce_scatter x2, waiting for transfers between devices, summed_rows(): subtotal = lax.psum_scatter(subtotal, axis, scatter_dimension=0, tiled=True)  18.3 us
    dot_general x35, matrix products, weighted(): jnp.einsum('hqk,khd->hqd', weights.astype(jnp.bfloat16), value_rows.resha...  17.2 us
  transfers between devices with their start and end apart: 6, of which 6 were waited for; matrix products, arithmetic and copies ran while one was open for 7% of the time, Pallas kernels for 0%

commit v1 on v0

v1 whole, which is shorter than its diff:
```python
import math

import jax
import jax.numpy as jnp
from jax import lax
from jax.experimental import pallas as pl
from jax.experimental.pallas import tpu as pltpu
from jax.sharding import Mesh
from jax.sharding import PartitionSpec as P

D = 3072
HD = 128
EPS = 1e-06
MESH = pl.DeviceIdType.MESH
AX = ("x", "zl", "c", "y", "zh")
ULY = ("y", "zh")
CHUNK = 48
ROWS = 8 * CHUNK
TXT = 16
KEYS = 2 * ROWS
QT = 256
LOG2 = math.log2(math.e) / math.sqrt(HD)
F32 = jnp.float32
BF16 = jnp.bfloat16


class Place:
    def __init__(self):
        self.x, self.zl, self.c, self.y, self.zh = (lax.axis_index(a) for a in AX)

    def at(self, **moved):
        found = {"x": self.x, "zl": self.zl, "c": self.c, "y": self.y, "zh": self.zh}
        found.update(moved)
        return found

    def group(self, dy, dz):
        y = lax.rem(self.y + dy, 4)
        if dz:
            return self.at(y=y, zh=1 - self.zh, zl=3 - self.zl)
        return self.at(y=y)

    def text_home(self):
        level = jnp.where(self.zh == 0, self.zl, 3 - self.zl)
        high = level // 2
        home = {"y": self.x, "zh": high, "zl": jnp.where(high == 0, level, 3 - level)}
        here = jnp.logical_and(self.y == self.x, self.zh == high)
        return home, here, lax.rem(level, 2)


GROUP = [(dy, dz) for dz in (0, 1) for dy in range(4) if (dy, dz) != (0, 0)]


def greet(devices, more=0):
    barrier = pltpu.get_barrier_semaphore()
    for device in devices:
        pl.semaphore_signal(barrier, inc=1, device_id=device, device_id_type=MESH)
    return lambda: pl.semaphore_wait(barrier, len(devices) + more)


def remote(src, dst, ssem, rsem, device):
    return pltpu.make_async_remote_copy(
        src_ref=src, dst_ref=dst, send_sem=ssem, recv_sem=rsem,
        device_id=device, device_id_type=MESH,
    )


def modulate(rows, factors):
    floats = rows.astype(F32)
    centre = floats - jnp.mean(floats, axis=-1, keepdims=True)
    spread = jnp.mean(centre * centre, axis=-1, keepdims=True)
    normed = centre / jnp.sqrt(spread + EPS)
    return (normed * (1.0 + factors[1:2].astype(F32)) + factors[0:1].astype(F32)).astype(BF16)


def head_norm(vectors, gain):
    inverse = lax.rsqrt(jnp.mean(vectors * vectors, axis=-1, keepdims=True) + EPS)
    return (vectors * inverse * gain).astype(BF16)


def project_kernel(
    xv, xt, mv, mt, gv, gt, wv_hbm, wt_hbm, qkv, tqkv,
    rows, trow, wv, wt, wsem, ssem, rsem, tssem, trsem,
):
    me = Place()
    load_v = pltpu.make_async_copy(wv_hbm, wv, wsem.at[0])
    load_t = pltpu.make_async_copy(
        wt_hbm.at[:, :, pl.ds(pl.multiple_of(me.c * HD, HD), HD)], wt, wsem.at[1]
    )
    load_v.start()
    load_t.start()
    arrived = greet([me.group(dy, dz) for dy, dz in GROUP])
    rows[0] = modulate(xv[...], mv[...])
    _, home, half = me.text_home()

    @pl.when(home)
    def _():
        trow[...] = modulate(xt[pl.ds(pl.multiple_of(half * TXT, TXT), TXT), :], mt[...])

    arrived()

    def copy(src, dst, device):
        return remote(rows.at[src], rows.at[dst], ssem.at[dst], rsem.at[dst], device)

    up, down = me.group(1, 0), me.group(3, 0)
    far_src = 3 - 2 * me.c
    far_device = me.at(y=lax.rem(me.y + 1 + 2 * me.c, 4))

    mirror = copy(0, 4, me.group(0, 1))
    mirror.start()

    def spread(base):
        low, high = copy(base, base + 1, down), copy(base, base + 3, up)

        @pl.when(me.c == 0)
        def _():
            high.start()
            low.start()

        @pl.when(me.c == 1)
        def _():
            low.start()
            high.start()

        return low, high

    def onward(base, low, high):
        far = copy(base + far_src, base + 2, far_device)

        @pl.when(me.c == 0)
        def _():
            high.wait_recv()
            far.start()
            low.wait_recv()

        @pl.when(me.c == 1)
        def _():
            low.wait_recv()
            far.start()
            high.wait_recv()

        return far

    text_copies = [
        remote(trow, trow, tssem.at[i], trsem, me.group(dy, dz)) for i, (dy, dz) in enumerate(GROUP)
    ]
    first = spread(0)

    @pl.when(home)
    def _():
        for text_copy in text_copies:
            text_copy.start()

    def block(p):
        lhs = rows[4 * p : 4 * p + 4].reshape(4 * CHUNK, D)
        for j in range(3):
            total = jnp.dot(lhs, wv[j], preferred_element_type=F32)
            for h in range(2):
                part = total[:, h * HD : (h + 1) * HD]
                part = head_norm(part, gv[j : j + 1]) if j < 2 else part.astype(BF16)
                qkv[h, j, p * 4 * CHUNK : (p + 1) * 4 * CHUNK, :] = part

    far0 = onward(0, *first)
    mirror.wait_recv()
    second = spread(4)
    load_v.wait()
    far0.wait_recv()
    block(0)
    far1 = onward(4, *second)

    @pl.when(jnp.logical_not(home))
    def _():
        text_copies[0].wait_recv()

    load_t.wait()
    for j in range(3):
        part = jnp.dot(trow[...], wt[j], preferred_element_type=F32)
        tqkv[j] = head_norm(part, gt[j : j + 1]) if j < 2 else part.astype(BF16)
    far1.wait_recv()
    block(1)
    for sent in (mirror, *first, far0, *second, far1):
        sent.wait_send()

    @pl.when(home)
    def _():
        for text_copy in text_copies:
            text_copy.wait_send()


def vmem(n):
    return [pl.BlockSpec(memory_space=pltpu.VMEM)] * n


def hbm(n):
    return [pl.BlockSpec(memory_space=pl.ANY)] * n


DMA = pltpu.SemaphoreType.DMA


def project(xv, xt, mv, mt, gv, gt, wv, wt):
    return pl.pallas_call(
        project_kernel,
        out_shape=(
            jax.ShapeDtypeStruct((2, 3, ROWS, HD), BF16),
            jax.ShapeDtypeStruct((3, TXT, HD), BF16),
        ),
        in_specs=vmem(6) + hbm(2),
        out_specs=tuple(vmem(2)),
        scratch_shapes=[
            pltpu.VMEM((8, CHUNK, D), BF16),
            pltpu.VMEM((TXT, D), BF16),
            pltpu.VMEM((3, D, 2 * HD), BF16),
            pltpu.VMEM((3, D, HD), BF16),
            DMA((2,)), DMA((8,)), DMA((8,)), DMA((7,)), DMA,
        ],
        compiler_params=pltpu.CompilerParams(collective_id=0, has_side_effects=True),
        name="project",
    )(xv, xt, mv, mt, gv, gt, wv, wt)


def attend_kernel(
    qkv, tqkv, heads, theads,
    qb, kvb, tq, mb, lb, ab, ob, sb, tob, orecv, srecv, trecv,
    kvs, kvr, qs, qr, tks, tkr, tqs, tqr, os_, or_, ss, sr, ts, tr,
):
    me = Place()
    c = me.c
    other = 1 - c
    peers = [me.at(c=other)]
    for d in range(1, 4):
        for r in (c, other):
            peers.append(me.at(x=lax.rem(me.x + d, 4), c=r))
            peers.append(me.at(zl=lax.rem(me.zl + d, 4), c=r))
    arrived = greet(peers)

    def at_rows(core):
        return pl.ds(pl.multiple_of(core * ROWS, ROWS), ROWS)

    sends = []

    def send(copy):
        copy.start()
        sends.append(copy)

    local = [
        pltpu.make_async_copy(qkv.at[c, pl.ds(1, 2)], kvb.at[0, :, at_rows(c), :], kvr.at[0, 0]),
        pltpu.make_async_copy(qkv.at[c, 0], qb.at[0, at_rows(c), :], qr.at[0, 0]),
        pltpu.make_async_copy(tqkv.at[pl.ds(1, 2)], kvb.at[2, :, pl.ds(KEYS, TXT), :], tkr.at[0]),
        pltpu.make_async_copy(tqkv.at[0], tq.at[pl.ds(0, TXT), :], tqr.at[0]),
    ]
    for copy in local:
        copy.start()
    mb[...] = jnp.full_like(mb, -jnp.inf)
    lb[...] = jnp.zeros_like(lb)
    ab[...] = jnp.zeros_like(ab)
    arrived()

    def send_kv(d, r, i):
        slot = (4 - d) % 4
        send(remote(
            qkv.at[r, pl.ds(1, 2)], kvb.at[slot, :, at_rows(c), :],
            kvs.at[slot, i], kvr.at[slot, i], me.at(x=lax.rem(me.x + d, 4), c=r),
        ))

    def send_q(d, r, i):
        slot = (4 - d) % 4
        send(remote(
            qkv.at[r, 0], qb.at[slot, at_rows(c), :],
            qs.at[slot, i], qr.at[slot, i], me.at(zl=lax.rem(me.zl + d, 4), c=r),
        ))

    send_kv(0, other, 1)
    send_q(0, other, 1)
    for d in (1, 3, 2):
        for i, r in enumerate((c, other)):
            send_q(d, r, i)
        slot = (4 - d) % 4
        send(remote(
            tqkv.at[0], tq.at[pl.ds(TXT * slot, TXT), :], tqs.at[slot], tqr.at[slot],
            me.at(zl=lax.rem(me.zl + d, 4)),
        ))
        for i, r in enumerate((c, other)):
            send_kv(d, r, i)
        send(remote(
            tqkv.at[pl.ds(1, 2)], kvb.at[2, :, pl.ds(KEYS + TXT * slot, TXT), :],
            tks.at[slot], tkr.at[slot], me.at(x=lax.rem(me.x + d, 4)),
        ))

    def await_kv(slot):
        for i in range(2):
            rows = kvb.at[slot, :, pl.ds(i * ROWS, ROWS), :]
            pltpu.make_async_copy(rows, rows, kvr.at[slot, i]).wait()

    def await_q(slot):
        for i in range(2):
            rows = qb.at[slot, pl.ds(i * ROWS, ROWS), :]
            pltpu.make_async_copy(rows, rows, qr.at[slot, i]).wait()

    def gray(i):
        return i + jnp.where(i == 2, 1, 0) - jnp.where(i == 3, 1, 0)

    def step(queries, slot, count, at):
        keys = kvb[slot, 0, :count, :]
        values = kvb[slot, 1, :count, :]
        scores = lax.dot_general(
            queries, keys, (((1,), (1,)), ((), ())), preferred_element_type=F32
        )
        before = mb[at, :]
        now = jnp.maximum(before[:, :1], jnp.max(scores, axis=-1, keepdims=True))
        weights = jnp.exp2((scores - now) * LOG2)
        shrink = jnp.exp2((before - now) * LOG2)
        totals = lb[at, :] * shrink + jnp.sum(weights, axis=-1, keepdims=True)
        sums = ab[at, :] * shrink + jnp.dot(
            weights.astype(BF16), values, preferred_element_type=F32
        )
        return jnp.broadcast_to(now, sums.shape), totals, sums

    def keep(at, state):
        mb[at, :], lb[at, :], ab[at, :] = state

    tail = pl.ds(4 * KEYS, 4 * TXT)
    tiles = KEYS // QT

    def phase(i, _):
        slot = gray(i)
        await_kv(slot)

        def tile(n, _):
            q_slot = gray(n // tiles)
            part = lax.rem(n, tiles)

            @pl.when(jnp.logical_and(i == 0, part == 0))
            def _():
                await_q(q_slot)

            at = pl.ds(pl.multiple_of(q_slot * KEYS + part * QT, QT), QT)
            inner = pl.ds(pl.multiple_of(part * QT, QT), QT)
            keep(at, step(qb[q_slot, inner, :], slot, KEYS, at))
            return 0

        lax.fori_loop(0, 4 * tiles, tile, 0)

        @pl.when(i == 0)
        def _():
            for j in range(4):
                rows = tq.at[pl.ds(j * TXT, TXT), :]
                pltpu.make_async_copy(rows, rows, tqr.at[j]).wait()

        keep(tail, step(tq[...], slot, KEYS, tail))
        return 0

    lax.fori_loop(0, 3, phase, 0)
    await_kv(2)
    for j in range(4):
        rows = kvb.at[2, :, pl.ds(KEYS + j * TXT, TXT), :]
        pltpu.make_async_copy(rows, rows, tkr.at[j]).wait()
    count = KEYS + 4 * TXT

    highest, totals, sums = step(tq[...], 2, count, tail)
    tob[:, :HD] = sums / totals
    tob[:, HD:] = highest * LOG2 + jnp.log2(totals)
    for j in range(4):
        slot = (4 - j) % 4
        for i, r in enumerate((c, other)):
            src, dst = tob.at[pl.ds(TXT * j, TXT), :], trecv.at[slot, c]
            if j == 0 and i == 0:
                mine_t = pltpu.make_async_copy(src, dst, tr.at[0, 0])
                mine_t.start()
            else:
                send(remote(src, dst, ts.at[slot, i], tr.at[slot, i],
                            me.at(zl=lax.rem(me.zl + j, 4), c=r)))

    def out_copies(j, slot, i, r):
        device = me.at(zl=lax.rem(me.zl + j, 4), c=r)
        at = pl.ds(pl.multiple_of(r * ROWS, ROWS), ROWS)
        return (
            remote(ob.at[j, at, :], orecv.at[slot, c], os_.at[slot, i], or_.at[slot, i], device),
            remote(sb.at[j, :, at], srecv.at[slot, c], ss.at[slot, i], sr.at[slot, i], device),
        )

    mine = (
        pltpu.make_async_copy(ob.at[0, at_rows(c), :], orecv.at[0, c], or_.at[0, 0]),
        pltpu.make_async_copy(sb.at[0, :, at_rows(c)], srecv.at[0, c], sr.at[0, 0]),
    )

    def last(n, _):
        q_slot = gray(3 - n // tiles)
        part = lax.rem(n, tiles)
        at = pl.ds(pl.multiple_of(q_slot * KEYS + part * QT, QT), QT)
        inner = pl.ds(pl.multiple_of(part * QT, QT), QT)
        highest, totals, sums = step(qb[q_slot, inner, :], 2, count, at)
        ob[q_slot, inner, :] = (sums / totals).astype(BF16)
        level = highest * LOG2 + jnp.log2(totals)
        sb[q_slot, :, inner] = jnp.transpose(level)[:8, :]

        @pl.when(jnp.logical_and(part == tiles - 1, q_slot > 0))
        def _():
            for i, r in enumerate((c, other)):
                for copy in out_copies(q_slot, 4 - q_slot, i, r):
                    copy.start()

        @pl.when(jnp.logical_and(part == tiles - 1, q_slot == 0))
        def _():
            for copy in out_copies(0, 0, 1, other):
                copy.start()
            for copy in mine:
                copy.start()

        return 0

    lax.fori_loop(0, 4 * tiles, last, 0)
    for copy in sends:
        copy.wait_send()
    for slot in range(4):
        for i, r in enumerate((c, other)):
            dst = trecv.at[slot, r]
            pltpu.make_async_copy(dst, dst, tr.at[slot, i]).wait()
    for h in range(2):
        found = [trecv[slot, h] for slot in range(4)]
        top = found[0][:, HD:]
        for part in found[1:]:
            top = jnp.maximum(top, part[:, HD:])
        weight = [jnp.exp2(part[:, HD:] - top) for part in found]
        mixed = sum(w * part[:, :HD] for w, part in zip(weight, found)) / sum(weight)
        theads[:, h * HD : (h + 1) * HD] = mixed.astype(BF16)
    for slot in range(4):
        for i, r in enumerate((c, other)):
            for dst, sems in ((orecv.at[slot, r], or_), (srecv.at[slot, r], sr)):
                pltpu.make_async_copy(dst, dst, sems.at[slot, i]).wait()
    for h in range(2):
        found = [srecv[slot, h] for slot in range(4)]
        top = jnp.maximum(jnp.maximum(found[0], found[1]), jnp.maximum(found[2], found[3]))
        weight = [jnp.exp2(part - top) for part in found]
        share = 1.0 / sum(weight)
        mixed = jnp.zeros((ROWS, HD), F32)
        for slot in range(4):
            row = (weight[slot] * share)[:1]
            column = jnp.transpose(jnp.broadcast_to(row, (HD, ROWS)))
            mixed = mixed + column * orecv[slot, h].astype(F32)
        heads[:, h * HD : (h + 1) * HD] = mixed.astype(BF16)
    for slot in range(4):
        for i, r in enumerate((c, other)):
            if (slot, i) != (0, 0):
                for copy in out_copies((4 - slot) % 4, slot, i, r):
                    copy.wait_send()


def attend(qkv, tqkv):
    return pl.pallas_call(
        attend_kernel,
        out_shape=(
            jax.ShapeDtypeStruct((ROWS, 2 * HD), BF16),
            jax.ShapeDtypeStruct((TXT, 2 * HD), BF16),
        ),
        in_specs=vmem(2),
        out_specs=tuple(vmem(2)),
        scratch_shapes=[
            pltpu.VMEM((4, KEYS, HD), BF16),
            pltpu.VMEM((4, 2, KEYS + 4 * TXT, HD), BF16),
            pltpu.VMEM((4 * TXT, HD), BF16),
            pltpu.VMEM((4 * KEYS + 4 * TXT, HD), F32),
            pltpu.VMEM((4 * KEYS + 4 * TXT, HD), F32),
            pltpu.VMEM((4 * KEYS + 4 * TXT, HD), F32),
            pltpu.VMEM((4, KEYS, HD), BF16),
            pltpu.VMEM((4, 8, KEYS), F32),
            pltpu.VMEM((4 * TXT, 2 * HD), F32),
            pltpu.VMEM((4, 2, ROWS, HD), BF16),
            pltpu.VMEM((4, 2, 8, ROWS), F32),
            pltpu.VMEM((4, 2, TXT, 2 * HD), F32),
        ]
        + [DMA((4, 2))] * 4 + [DMA((4,))] * 4 + [DMA((4, 2))] * 6,
        compiler_params=pltpu.CompilerParams(collective_id=1, has_side_effects=True),
        name="attend",
    )(qkv, tqkv)


def finish_kernel(
    heads, theads, mv, mt, wv_hbm, wt_hbm, video_out, text_out,
    pb, fb, nb, zb, zs, tp, trb, tfin, tpiece, wv, wt,
    wsem, fs, fr, ns, nr, zsem, zr, tss, trs, bs, br,
):
    me = Place()
    c = me.c
    half_cols = D // 2
    load_v = pltpu.make_async_copy(wv_hbm, wv, wsem.at[0])
    cols = pl.ds(pl.multiple_of(c * half_cols, half_cols), half_cols)
    load_t = pltpu.make_async_copy(wt_hbm.at[:, cols], wt, wsem.at[1])
    load_v.start()
    load_t.start()
    lin = (me.x * 4 + me.zl) * 2 + c

    def plane(k):
        n = lax.rem(lin + k, 32)
        return me.at(x=n // 8, zl=lax.rem(n // 2, 4), c=lax.rem(n, 2))

    arrived = greet([me.group(dy, dz) for dy, dz in GROUP], 31)
    barrier = pltpu.get_barrier_semaphore()

    def hello(k, _):
        pl.semaphore_signal(barrier, inc=1, device_id=plane(k), device_id_type=MESH)
        return 0

    lax.fori_loop(1, 32, hello, 0)
    home_at, home, _ = me.text_home()
    mine = me.y * 2 + me.zh

    load_t.wait()
    part = jnp.dot(theads[...], wt[...], preferred_element_type=F32).astype(BF16)
    tp[...] = part
    load_v.wait()
    for p in (1, 0):
        lhs = heads[p * 4 * CHUNK : (p + 1) * 4 * CHUNK, :]
        for q in range(4):
            span = slice(q * (D // 4), (q + 1) * (D // 4))
            found = jnp.dot(lhs, wv[:, span], preferred_element_type=F32).astype(BF16)
            pb[4 * p : 4 * p + 4, :, span] = found.reshape(4, CHUNK, D // 4)
    arrived()

    gather_text = remote(tp, trb.at[mine], tss.at[0], trs.at[mine], me.at(**home_at))

    @pl.when(jnp.logical_not(home))
    def _():
        gather_text.start()

    up, down = me.group(1, 0), me.group(3, 0)
    far_device = me.at(y=lax.rem(me.y + 3 + 2 * c, 4))
    near_device = far_device
    near_slot = 3 - 2 * c
    plain_device = me.at(y=lax.rem(me.y + 1 + 2 * c, 4))
    plain_slot = 1 + 2 * c

    def far_copy(p):
        return remote(pb.at[4 * p + 2], fb.at[p], fs.at[p], fr.at[p], far_device)

    def plain_copy(p):
        return remote(pb.at[4 * p + plain_slot], nb.at[p, 0], ns.at[p, 0], nr.at[p, 0], plain_device)

    def sum_copy(p):
        return remote(pb.at[4 * p + near_slot], nb.at[p, 1], ns.at[p, 1], nr.at[p, 1], near_device)

    for p in (1, 0):
        far_copy(p).start()
        plain_copy(p).start()

    def relay(p):
        far_copy(p).wait_recv()
        total = pb[4 * p + near_slot].astype(F32) + fb[p].astype(F32)
        pb[4 * p + near_slot] = total.astype(BF16)
        sum_copy(p).start()

    def collect(p):
        plain_copy(p).wait_recv()
        sum_copy(p).wait_recv()
        return pb[4 * p].astype(F32) + nb[p, 0].astype(F32) + nb[p, 1].astype(F32)

    mirror = remote(zs, zb, zsem, zr, me.group(0, 1))
    relay(1)
    zs[...] = collect(1).astype(BF16)
    mirror.start()

    level = jnp.where(me.zh == 0, me.zl, 3 - me.zl)

    def piece_copy(k):
        return remote(
            tfin, tpiece.at[lax.rem(level, 2), c],
            bs.at[k - 1], br.at[lax.rem(level, 2), c], plane(k),
        )

    @pl.when(home)
    def _():
        total = tp[...].astype(F32)
        for s in range(8):
            @pl.when(s != mine)
            def _():
                pltpu.make_async_copy(trb.at[s], trb.at[s], trs.at[s]).wait()

            @pl.when(s == mine)
            def _():
                trb[s] = tp[...]

        total = trb[0].astype(F32)
        for s in range(1, 8):
            total = total + trb[s].astype(F32)
        gate = mt[2:3, cols].astype(F32)
        tfin[...] = (total * gate).astype(BF16)

        def out(k, _):
            piece_copy(k).start()
            return 0

        lax.fori_loop(1, 32, out, 0)
        tpiece[lax.rem(level, 2), c] = tfin[...]

    relay(0)
    summed = collect(0)
    mirror.wait_recv()
    summed = summed + zb[...].astype(F32)
    video_out[...] = (summed * mv[2:3].astype(F32)).astype(BF16)

    for b in range(2):
        for r in range(2):
            @pl.when(jnp.logical_not(jnp.logical_and(home, jnp.logical_and(lax.rem(level, 2) == b, c == r))))
            def _():
                pltpu.make_async_copy(tpiece.at[b, r], tpiece.at[b, r], br.at[b, r]).wait()
            text_out[b * TXT : (b + 1) * TXT, r * half_cols : (r + 1) * half_cols] = tpiece[b, r]
    for p in (0, 1):
        far_copy(p).wait_send()
        plain_copy(p).wait_send()
        sum_copy(p).wait_send()
    mirror.wait_send()

    @pl.when(jnp.logical_not(home))
    def _():
        gather_text.wait_send()

    @pl.when(home)
    def _():
        def done(k, _):
            piece_copy(k).wait_send()
            return 0

        lax.fori_loop(1, 32, done, 0)


def finish(heads, theads, mv, mt, wv, wt):
    half_cols = D // 2
    return pl.pallas_call(
        finish_kernel,
        out_shape=(
            jax.ShapeDtypeStruct((CHUNK, D), BF16),
            jax.ShapeDtypeStruct((2 * TXT, D), BF16),
        ),
        in_specs=vmem(4) + hbm(2),
        out_specs=tuple(vmem(2)),
        scratch_shapes=[
            pltpu.VMEM((8, CHUNK, D), BF16),
            pltpu.VMEM((2, CHUNK, D), BF16),
            pltpu.VMEM((2, 2, CHUNK, D), BF16),
            pltpu.VMEM((CHUNK, D), BF16),
            pltpu.VMEM((CHUNK, D), BF16),
            pltpu.VMEM((TXT, half_cols), BF16),
            pltpu.VMEM((8, TXT, half_cols), BF16),
            pltpu.VMEM((TXT, half_cols), BF16),
            pltpu.VMEM((2, 2, TXT, half_cols), BF16),
            pltpu.VMEM((2 * HD, D), BF16),
            pltpu.VMEM((2 * HD, half_cols), BF16),
            DMA((2,)), DMA((2,)), DMA((2,)), DMA((2, 2)), DMA((2, 2)), DMA, DMA,
            DMA((1,)), DMA((8,)), DMA((31,)), DMA((2, 2)),
        ],
        compiler_params=pltpu.CompilerParams(collective_id=2, has_side_effects=True),
        name="finish",
    )(heads, theads, mv, mt, wv, wt)


def local(
    video_tokens, text_tokens, video_modulation, text_modulation, video_projection,
    text_projection, video_output, text_output, video_gains, text_gains,
):
    qkv, tqkv = project(
        video_tokens, text_tokens, video_modulation, text_modulation, video_gains, text_gains,
        jnp.transpose(video_projection, (1, 0, 2)), jnp.transpose(text_projection, (1, 0, 2)),
    )
    heads, theads = attend(qkv, tqkv)
    return finish(heads, theads, video_modulation, text_modulation, video_output, text_output)


def solution(mesh):
    torus = Mesh(mesh.devices.reshape(4, 4, 2, 4, 2), AX)
    placed = (
        P(AX, None),
        P(ULY, None),
        P(),
        P(),
        P(None, None, ULY),
        P(None, None, ULY),
        P(ULY, None),
        P(ULY, None),
        P(),
        P(),
    )
    return jax.shard_map(
        local,
        mesh=torus,
        in_specs=placed,
        out_specs=(P(AX, None), P(ULY, None)),
        check_vma=False,
    )
```

time: 412 us -> 183 us (0.44)
  waiting for transfers between devices: 249 us -> 0 us
  Pallas kernels: 0 us -> 177 us
  matrix products: 46.4 us -> 0 us
  local copies, waits for them, and re-layouts: 43.2 us -> 3.31 us
  blocking collectives: 30 us -> 0 us
  other arithmetic: 18.7 us -> 0 us
  between operations: 14.3 us -> 0.66 us
  starting transfers between devices: 6.67 us -> 0 us
    all_gather x3 -> x0, waiting for transfers between devices: 197 us -> none  [the longest x1 81 us: local(): lax.all_gather(modulate(video_tokens, video_modulation), ULY, axis=0, til...]
    pallas_call x0 -> x3, Pallas kernels: none -> 177 us  [the longest x1 77.9 us: attend(): pl.pallas_call(attend_kernel, out_shape=(jax.ShapeDtypeStruct((ROWS, 2 *...]
    dot_general x74 -> x0, matrix products: 46.4 us -> none  [the longest x35 17.2 us: weighted(): jnp.einsum('hqk,khd->hqd', weights.astype(jnp.bfloat16), value_rows.resha...]
    slice x39 -> x0, local copies, waits for them, and re-layouts: 38 us -> none  [the longest x32 34.2 us: one_turn(): return absorb(inner_state, query_rows, sliced[:, 0], sliced[:, 1])]
    all_to_all x1 -> x0, waiting for transfers between devices: 33.4 us -> none  [summed_on_arrival(): tiles = lax.all_to_all(split_up(x, dim, length), axis, 0, 0, tiled=True)]
    all_gather x3 -> x0, blocking collectives: 30 us -> none  [collected_together(): both, at, found = (lax.all_gather(jnp.concatenate(lines), axis), 0, {})]
    reduce_scatter x2 -> x0, waiting for transfers between devices: 18.3 us -> none  [summed_rows(): subtotal = lax.psum_scatter(subtotal, axis, scatter_dimension=0, tiled=True)]
    reduce_sum x44 -> x0, other arithmetic: 9.79 us -> none  [the longest x33 5.8 us: absorb(): jnp.sum(weights, axis=-1)]
  transfers between devices with their start and end apart: 6 -> 0, of which waited for: 6 -> 0; matrix products, arithmetic and copies ran while one was open for 7% -> 0% of each run, Pallas kernels for 0% -> 0%
where the time goes in v1:
time: 183 us; the launch traced here: 181 us
  Pallas kernels  177 us (97%)
  local copies, waits for them, and re-layouts  3.31 us (2%)
    pallas_call x1, Pallas kernels, attend(): pl.pallas_call(attend_kernel, out_shape=(jax.ShapeDtypeStruct((ROWS, 2 *...  77.9 us
    pallas_call x1, Pallas kernels, finish(): pl.pallas_call(finish_kernel, out_shape=(jax.ShapeDtypeStruct((CHUNK, D),...  59.3 us
    pallas_call x1, Pallas kernels, project(): pl.pallas_call(project_kernel, out_shape=(jax.ShapeDtypeStruct((2, 3, ROW...  40.2 us

profile of v1, /device:TPU:1, one launch (start us, length us, event | category | flops | bytes accessed | tf_op | source)
XLA Modules:
  0.0 181.4 jit_solution(10881467295796130518)
XLA Ops:
  0.6 40.2 %project.1 = (bf16[2,3,384,128]{3,2,1,0:T(8,128)(2,1)}, bf16[3,16,128]{2,1,0:T(8,128)(2,1)}) custom-call(bf16[48,3072]{1,0:T(8,128)(2,1)} %xv.1, bf16[32,3072]{1,0:T(8,128)(2,1)} %xt.1, bf16[3,3072]{1,0:T(4,128)(2,1)} %mv.3, bf16[3,3072]{1,0:T(4,128)(2,1)} %mt.3, f32[2,128]{1,0:T(2,128)} %gv.1, f32[2,128]{1,0:T(2,128)} %gt.1, bf16[3,3072,256]{2,1,0:T(8,128)(2,1)} %bitcast.2, ...), custom_call_target="tpu_custom_call" | custom-call | tf_op jit(solution)/shard_map/project/pallas_call | solution.py:201
  40.8 77.9 %attend.1 = (bf16[384,256]{1,0:T(8,128)(2,1)}, bf16[16,256]{1,0:T(8,128)(2,1)}) custom-call(bf16[2,3,384,128]{3,2,1,0:T(8,128)(2,1)} %get-tuple-element.6.qkv, bf16[3,16,128]{2,1,0:T(8,128)(2,1)} %get-tuple-element.7.tqkv), custom_call_target="tpu_custom_call" | custom-call | tf_op jit(solution)/shard_map/attend/pallas_call | solution.py:449
  118.7 59.3 %finish.1 = (bf16[48,3072]{1,0:T(8,128)(2,1)}, bf16[32,3072]{1,0:T(8,128)(2,1)}) custom-call(bf16[384,256]{1,0:T(8,128)(2,1)} %get-tuple-element.8.heads, bf16[16,256]{1,0:T(8,128)(2,1)} %get-tuple-element.9.theads, bf16[3,3072]{1,0:T(4,128)(2,1)} %mv.3, bf16[3,3072]{1,0:T(4,128)(2,1)} %mt.3, bf16[256,3072]{1,0:T(8,128)(2,1)} %wv_hbm.1, bf16[256,3072]{1,0:T(8,128)(2,1)} %wt_hbm.1), custom_call_target="tpu_custom_call" | custom-call | tf_op jit(solution)/shard_map/finish/pallas_call | solution.py:627
  178.0 1.7 copy.14
  179.7 1.6 copy.15

commit v2 on v1

--- a/solution.py
+++ b/solution.py
@@ -18,7 +18,7 @@
 ROWS = 8 * CHUNK
 TXT = 16
 KEYS = 2 * ROWS
-QT = 256
+QT = 384
 LOG2 = math.log2(math.e) / math.sqrt(HD)
 F32 = jnp.float32
 BF16 = jnp.bfloat16
@@ -39,12 +39,8 @@
             return self.at(y=y, zh=1 - self.zh, zl=3 - self.zl)
         return self.at(y=y)
 
-    def text_home(self):
-        level = jnp.where(self.zh == 0, self.zl, 3 - self.zl)
-        high = level // 2
-        home = {"y": self.x, "zh": high, "zl": jnp.where(high == 0, level, 3 - level)}
-        here = jnp.logical_and(self.y == self.x, self.zh == high)
-        return home, here, lax.rem(level, 2)
+    def piece(self):
+        return lax.rem(self.y + self.x, 4), jnp.where(self.zl < 2, self.zh, 1 - self.zh), lax.rem(self.zl, 2)
 
 
 GROUP = [(dy, dz) for dz in (0, 1) for dy in range(4) if (dy, dz) != (0, 0)]
@@ -79,7 +75,7 @@
 
 def project_kernel(
     xv, xt, mv, mt, gv, gt, wv_hbm, wt_hbm, qkv, tqkv,
-    rows, trow, wv, wt, wsem, ssem, rsem, tssem, trsem,
+    rows, ttmp, trow, wv, wt, wsem, ssem, rsem, tssem, trsem,
 ):
     me = Place()
     load_v = pltpu.make_async_copy(wv_hbm, wv, wsem.at[0])
@@ -90,11 +86,17 @@
     load_t.start()
     arrived = greet([me.group(dy, dz) for dy, dz in GROUP])
     rows[0] = modulate(xv[...], mv[...])
-    _, home, half = me.text_home()
-
-    @pl.when(home)
-    def _():
-        trow[...] = modulate(xt[pl.ds(pl.multiple_of(half * TXT, TXT), TXT), :], mt[...])
+    low_chip = me.zl < 2
+    stays = jnp.logical_and(low_chip, me.x == 0)
+
+    @pl.when(low_chip)
+    def _():
+        for b in range(2):
+            ttmp[b] = modulate(xt[b * TXT : (b + 1) * TXT, :], mt[...])
+
+    @pl.when(stays)
+    def _():
+        trow[...] = ttmp[me.zl]
 
     arrived()
 
@@ -140,15 +142,21 @@
 
         return far
 
-    text_copies = [
-        remote(trow, trow, tssem.at[i], trsem, me.group(dy, dz)) for i, (dy, dz) in enumerate(GROUP)
-    ]
+    text_y = lax.rem(me.y + 4 - me.x, 4)
+    text_near = remote(ttmp.at[lax.rem(me.zl, 2)], trow, tssem.at[0], trsem, me.at(y=text_y))
+    text_over = remote(
+        ttmp.at[1 - lax.rem(me.zl, 2)], trow, tssem.at[1], trsem,
+        me.at(y=text_y, zh=1 - me.zh, zl=3 - me.zl),
+    )
     first = spread(0)
 
-    @pl.when(home)
-    def _():
-        for text_copy in text_copies:
-            text_copy.start()
+    @pl.when(low_chip)
+    def _():
+        text_over.start()
+
+    @pl.when(jnp.logical_and(low_chip, me.x > 0))
+    def _():
+        text_near.start()
 
     def block(p):
         lhs = rows[4 * p : 4 * p + 4].reshape(4 * CHUNK, D)
@@ -167,9 +175,9 @@
     block(0)
     far1 = onward(4, *second)
 
-    @pl.when(jnp.logical_not(home))
-    def _():
-        text_copies[0].wait_recv()
+    @pl.when(jnp.logical_not(stays))
+    def _():
+        text_near.wait_recv()
 
     load_t.wait()
     for j in range(3):
@@ -180,10 +188,13 @@
     for sent in (mirror, *first, far0, *second, far1):
         sent.wait_send()
 
-    @pl.when(home)
-    def _():
-        for text_copy in text_copies:
-            text_copy.wait_send()
+    @pl.when(low_chip)
+    def _():
+        text_over.wait_send()
+
+    @pl.when(jnp.logical_and(low_chip, me.x > 0))
+    def _():
+        text_near.wait_send()
 
 
 def vmem(n):
@@ -208,10 +219,11 @@
         out_specs=tuple(vmem(2)),
         scratch_shapes=[
             pltpu.VMEM((8, CHUNK, D), BF16),
+            pltpu.VMEM((2, TXT, D), BF16),
             pltpu.VMEM((TXT, D), BF16),
             pltpu.VMEM((3, D, 2 * HD), BF16),
             pltpu.VMEM((3, D, HD), BF16),
-            DMA((2,)), DMA((8,)), DMA((8,)), DMA((7,)), DMA,
+            DMA((2,)), DMA((8,)), DMA((8,)), DMA((2,)), DMA,
         ],
         compiler_params=pltpu.CompilerParams(collective_id=0, has_side_effects=True),
         name="project",
@@ -220,7 +232,7 @@
 
 def attend_kernel(
     qkv, tqkv, heads, theads,
-    qb, kvb, tq, mb, lb, ab, ob, sb, tob, orecv, srecv, trecv,
+    qb, kva, kvb, tq, mb, lb, ab, ob, sb, tob, orecv, srecv, trecv,
     kvs, kvr, qs, qr, tks, tkr, tqs, tqr, os_, or_, ss, sr, ts, tr,
 ):
     me = Place()
@@ -242,23 +254,28 @@
         copy.start()
         sends.append(copy)
 
+    def kv_rows(slot, core):
+        buf = kva if slot in (0, 1) else kvb
+        base = 0 if slot in (0, 3) else KEYS
+        return buf.at[:, pl.ds(pl.multiple_of(base + core * ROWS, ROWS), ROWS), :]
+
+    def kv_text(slot):
+        return kvb.at[:, pl.ds(2 * KEYS + TXT * slot, TXT), :]
+
     local = [
-        pltpu.make_async_copy(qkv.at[c, pl.ds(1, 2)], kvb.at[0, :, at_rows(c), :], kvr.at[0, 0]),
+        pltpu.make_async_copy(qkv.at[c, pl.ds(1, 2)], kv_rows(0, c), kvr.at[0, 0]),
         pltpu.make_async_copy(qkv.at[c, 0], qb.at[0, at_rows(c), :], qr.at[0, 0]),
-        pltpu.make_async_copy(tqkv.at[pl.ds(1, 2)], kvb.at[2, :, pl.ds(KEYS, TXT), :], tkr.at[0]),
+        pltpu.make_async_copy(tqkv.at[pl.ds(1, 2)], kv_text(0), tkr.at[0]),
         pltpu.make_async_copy(tqkv.at[0], tq.at[pl.ds(0, TXT), :], tqr.at[0]),
     ]
     for copy in local:
         copy.start()
-    mb[...] = jnp.full_like(mb, -jnp.inf)
-    lb[...] = jnp.zeros_like(lb)
-    ab[...] = jnp.zeros_like(ab)
     arrived()
 
     def send_kv(d, r, i):
         slot = (4 - d) % 4
         send(remote(
-            qkv.at[r, pl.ds(1, 2)], kvb.at[slot, :, at_rows(c), :],
+            qkv.at[r, pl.ds(1, 2)], kv_rows(slot, c),
             kvs.at[slot, i], kvr.at[slot, i], me.at(x=lax.rem(me.x + d, 4), c=r),
         ))
 
@@ -271,7 +288,7 @@
 
     send_kv(0, other, 1)
     send_q(0, other, 1)
-    for d in (1, 3, 2):
+    for d in (3, 1, 2):
         for i, r in enumerate((c, other)):
             send_q(d, r, i)
         slot = (4 - d) % 4
@@ -282,13 +299,13 @@
         for i, r in enumerate((c, other)):
             send_kv(d, r, i)
         send(remote(
-            tqkv.at[pl.ds(1, 2)], kvb.at[2, :, pl.ds(KEYS + TXT * slot, TXT), :],
+            tqkv.at[pl.ds(1, 2)], kv_text(slot),
             tks.at[slot], tkr.at[slot], me.at(x=lax.rem(me.x + d, 4)),
         ))
 
     def await_kv(slot):
         for i in range(2):
-            rows = kvb.at[slot, :, pl.ds(i * ROWS, ROWS), :]
+            rows = kv_rows(slot, i)
             pltpu.make_async_copy(rows, rows, kvr.at[slot, i]).wait()
 
     def await_q(slot):
@@ -299,66 +316,70 @@
     def gray(i):
         return i + jnp.where(i == 2, 1, 0) - jnp.where(i == 3, 1, 0)
 
-    def step(queries, slot, count, at):
-        keys = kvb[slot, 0, :count, :]
-        values = kvb[slot, 1, :count, :]
-        scores = lax.dot_general(
+    def scored(queries, keys):
+        return lax.dot_general(
             queries, keys, (((1,), (1,)), ((), ())), preferred_element_type=F32
         )
+
+    def lanes(weights):
+        width = weights.shape[1]
+        if width % HD:
+            extra = weights[:, width - width % HD :]
+            pad = jnp.zeros((extra.shape[0], HD - width % HD), F32)
+            total = jnp.concatenate([extra, pad], axis=1)
+        else:
+            total = jnp.zeros((weights.shape[0], HD), F32)
+        for k in range(width // HD):
+            total = total + weights[:, k * HD : (k + 1) * HD]
+        return total
+
+    def open_step(queries, at):
+        scores = scored(queries, kva[0])
+        now = jnp.max(scores, axis=-1, keepdims=True)
+        weights = jnp.exp2((scores - now) * LOG2)
+        mb[at, :] = jnp.broadcast_to(now, (queries.shape[0], HD))
+        lb[at, :] = lanes(weights)
+        ab[at, :] = jnp.dot(weights.astype(BF16), kva[1], preferred_element_type=F32)
+
+    def last_step(queries, at):
+        scores = scored(queries, kvb[0])
         before = mb[at, :]
         now = jnp.maximum(before[:, :1], jnp.max(scores, axis=-1, keepdims=True))
         weights = jnp.exp2((scores - now) * LOG2)
         shrink = jnp.exp2((before - now) * LOG2)
-        totals = lb[at, :] * shrink + jnp.sum(weights, axis=-1, keepdims=True)
+        totals = jnp.sum(lb[at, :] * shrink + lanes(weights), axis=-1, keepdims=True)
         sums = ab[at, :] * shrink + jnp.dot(
-            weights.astype(BF16), values, preferred_element_type=F32
+            weights.astype(BF16), kvb[1], preferred_element_type=F32
         )
-        return jnp.broadcast_to(now, sums.shape), totals, sums
-
-    def keep(at, state):
-        mb[at, :], lb[at, :], ab[at, :] = state
+        level = jnp.broadcast_to(now * LOG2 + jnp.log2(totals), sums.shape)
+        return sums / totals, level
 
     tail = pl.ds(4 * KEYS, 4 * TXT)
-    tiles = KEYS // QT
-
-    def phase(i, _):
-        slot = gray(i)
-        await_kv(slot)
-
-        def tile(n, _):
-            q_slot = gray(n // tiles)
-            part = lax.rem(n, tiles)
-
-            @pl.when(jnp.logical_and(i == 0, part == 0))
-            def _():
-                await_q(q_slot)
-
+
+    await_kv(0)
+    await_kv(1)
+
+    def open_slot(i, _):
+        q_slot = gray(i)
+        await_q(q_slot)
+        for part in range(KEYS // QT):
             at = pl.ds(pl.multiple_of(q_slot * KEYS + part * QT, QT), QT)
-            inner = pl.ds(pl.multiple_of(part * QT, QT), QT)
-            keep(at, step(qb[q_slot, inner, :], slot, KEYS, at))
-            return 0
-
-        lax.fori_loop(0, 4 * tiles, tile, 0)
-
-        @pl.when(i == 0)
-        def _():
-            for j in range(4):
-                rows = tq.at[pl.ds(j * TXT, TXT), :]
-                pltpu.make_async_copy(rows, rows, tqr.at[j]).wait()
-
-        keep(tail, step(tq[...], slot, KEYS, tail))
+            open_step(qb[q_slot, part * QT : (part + 1) * QT, :], at)
         return 0
 
-    lax.fori_loop(0, 3, phase, 0)
+    lax.fori_loop(0, 4, open_slot, 0)
+    for j in range(4):
+        rows = tq.at[pl.ds(j * TXT, TXT), :]
+        pltpu.make_async_copy(rows, rows, tqr.at[j]).wait()
+    open_step(tq[...], tail)
+    await_kv(3)
     await_kv(2)
     for j in range(4):
-        rows = kvb.at[2, :, pl.ds(KEYS + j * TXT, TXT), :]
-        pltpu.make_async_copy(rows, rows, tkr.at[j]).wait()
-    count = KEYS + 4 * TXT
-
-    highest, totals, sums = step(tq[...], 2, count, tail)
-    tob[:, :HD] = sums / totals
-    tob[:, HD:] = highest * LOG2 + jnp.log2(totals)
+        pltpu.make_async_copy(kv_text(j), kv_text(j), tkr.at[j]).wait()
+
+    mixed, level = last_step(tq[...], tail)
+    tob[:, :HD] = mixed
+    tob[:, HD:] = level
     for j in range(4):
         slot = (4 - j) % 4
         for i, r in enumerate((c, other)):
@@ -383,23 +404,22 @@
         pltpu.make_async_copy(sb.at[0, :, at_rows(c)], srecv.at[0, c], sr.at[0, 0]),
     )
 
-    def last(n, _):
-        q_slot = gray(3 - n // tiles)
-        part = lax.rem(n, tiles)
-        at = pl.ds(pl.multiple_of(q_slot * KEYS + part * QT, QT), QT)
-        inner = pl.ds(pl.multiple_of(part * QT, QT), QT)
-        highest, totals, sums = step(qb[q_slot, inner, :], 2, count, at)
-        ob[q_slot, inner, :] = (sums / totals).astype(BF16)
-        level = highest * LOG2 + jnp.log2(totals)
-        sb[q_slot, :, inner] = jnp.transpose(level)[:8, :]
-
-        @pl.when(jnp.logical_and(part == tiles - 1, q_slot > 0))
+    def last_slot(n, _):
+        q_slot = gray(3 - n)
+        for part in range(KEYS // QT):
+            at = pl.ds(pl.multiple_of(q_slot * KEYS + part * QT, QT), QT)
+            inner = slice(part * QT, (part + 1) * QT)
+            mixed, level = last_step(qb[q_slot, inner, :], at)
+            ob[q_slot, inner, :] = mixed.astype(BF16)
+            sb[q_slot, :, inner] = jnp.transpose(level)[:8, :]
+
+        @pl.when(q_slot > 0)
         def _():
             for i, r in enumerate((c, other)):
                 for copy in out_copies(q_slot, 4 - q_slot, i, r):
                     copy.start()
 
-        @pl.when(jnp.logical_and(part == tiles - 1, q_slot == 0))
+        @pl.when(q_slot == 0)
         def _():
             for copy in out_copies(0, 0, 1, other):
                 copy.start()
@@ -408,7 +428,7 @@
 
         return 0
 
-    lax.fori_loop(0, 4 * tiles, last, 0)
+    lax.fori_loop(0, 4, last_slot, 0)
     for copy in sends:
         copy.wait_send()
     for slot in range(4):
@@ -456,7 +476,8 @@
         out_specs=tuple(vmem(2)),
         scratch_shapes=[
             pltpu.VMEM((4, KEYS, HD), BF16),
-            pltpu.VMEM((4, 2, KEYS + 4 * TXT, HD), BF16),
+            pltpu.VMEM((2, 2 * KEYS, HD), BF16),
+            pltpu.VMEM((2, 2 * KEYS + 4 * TXT, HD), BF16),
             pltpu.VMEM((4 * TXT, HD), BF16),
             pltpu.VMEM((4 * KEYS + 4 * TXT, HD), F32),
             pltpu.VMEM((4 * KEYS + 4 * TXT, HD), F32),
@@ -476,8 +497,8 @@
 
 def finish_kernel(
     heads, theads, mv, mt, wv_hbm, wt_hbm, video_out, text_out,
-    pb, fb, nb, zb, zs, tp, trb, tfin, tpiece, wv, wt,
-    wsem, fs, fr, ns, nr, zsem, zr, tss, trs, bs, br,
+    pb, fb, nb, zb, zs, tp, trb, tfin, tall, wv, wt,
+    wsem, fs, fr, ns, nr, zsem, zr, tss, trs, bs, br, xs, xr,
 ):
     me = Place()
     c = me.c
@@ -487,26 +508,39 @@
     load_t = pltpu.make_async_copy(wt_hbm.at[:, cols], wt, wsem.at[1])
     load_v.start()
     load_t.start()
-    lin = (me.x * 4 + me.zl) * 2 + c
-
-    def plane(k):
-        n = lax.rem(lin + k, 32)
-        return me.at(x=n // 8, zl=lax.rem(n // 2, 4), c=lax.rem(n, 2))
-
-    arrived = greet([me.group(dy, dz) for dy, dz in GROUP], 31)
+    piece_y, piece_zh, half = me.piece()
+    mine = me.y * 2 + me.zh
+    home = me.zl // 2 == c
+
+    def gatherer(k):
+        return me.at(x=k, zl=2 * c + half, y=piece_y, zh=piece_zh)
+
+    def giver(s):
+        y, zh = s // 2, s % 2
+        side = jnp.where(me.zh == zh, 0, 1)
+        return me.at(x=lax.rem(me.y + 4 - y, 4), zl=2 * side + half, y=y, zh=zh)
+
+    own_piece = jnp.logical_and(me.x == 0, jnp.logical_and(me.zl < 2, c == 0))
+    column = [me.at(zl=lax.rem(me.zl + d, 4), c=r) for d in range(4) for r in (c, 1 - c)]
+    across = [me.at(x=lax.rem(me.x + d, 4)) for d in range(1, 4)]
+    up, down = me.group(1, 0), me.group(3, 0)
+    arrived = greet(
+        [up, down, me.group(0, 1)] + column[1:] + across,
+        4 - jnp.where(own_piece, 1, 0),
+    )
     barrier = pltpu.get_barrier_semaphore()
 
-    def hello(k, _):
-        pl.semaphore_signal(barrier, inc=1, device_id=plane(k), device_id_type=MESH)
-        return 0
-
-    lax.fori_loop(1, 32, hello, 0)
-    home_at, home, _ = me.text_home()
-    mine = me.y * 2 + me.zh
+    @pl.when(home)
+    def _():
+        for s in range(8):
+            @pl.when(jnp.logical_not(jnp.logical_and(own_piece, s == mine)))
+            def _():
+                pl.semaphore_signal(barrier, inc=1, device_id=giver(s), device_id_type=MESH)
 
     load_t.wait()
     part = jnp.dot(theads[...], wt[...], preferred_element_type=F32).astype(BF16)
-    tp[...] = part
+    for k in range(4):
+        tp[k] = part[:, k * (D // 8) : (k + 1) * (D // 8)]
     load_v.wait()
     for p in (1, 0):
         lhs = heads[p * 4 * CHUNK : (p + 1) * 4 * CHUNK, :]
@@ -516,13 +550,21 @@
             pb[4 * p : 4 * p + 4, :, span] = found.reshape(4, CHUNK, D // 4)
     arrived()
 
-    gather_text = remote(tp, trb.at[mine], tss.at[0], trs.at[mine], me.at(**home_at))
-
-    @pl.when(jnp.logical_not(home))
-    def _():
-        gather_text.start()
-
-    up, down = me.group(1, 0), me.group(3, 0)
+    text_parts = [
+        remote(tp.at[k], trb.at[mine], tss.at[k], trs.at[mine], gatherer(k)) for k in range(4)
+    ]
+    own_part = pltpu.make_async_copy(tp.at[0], trb.at[mine], trs.at[mine])
+
+    @pl.when(own_piece)
+    def _():
+        own_part.start()
+
+    @pl.when(jnp.logical_not(own_piece))
+    def _():
+        text_parts[0].start()
+
+    for text_part in text_parts[1:]:
+        text_part.start()
     far_device = me.at(y=lax.rem(me.y + 3 + 2 * c, 4))
     near_device = far_device
     near_slot = 3 - 2 * c
@@ -558,68 +600,67 @@
     zs[...] = collect(1).astype(BF16)
     mirror.start()
 
-    level = jnp.where(me.zh == 0, me.zl, 3 - me.zl)
-
-    def piece_copy(k):
-        return remote(
-            tfin, tpiece.at[lax.rem(level, 2), c],
-            bs.at[k - 1], br.at[lax.rem(level, 2), c], plane(k),
-        )
+    shares = [
+        remote(tfin, tall.at[me.x, half, c], bs.at[i], br.at[half, c], device)
+        for i, device in enumerate(column[1:])
+    ]
 
     @pl.when(home)
     def _():
-        total = tp[...].astype(F32)
+        total = jnp.zeros((TXT, D // 8), F32)
         for s in range(8):
-            @pl.when(s != mine)
+            pltpu.make_async_copy(trb.at[s], trb.at[s], trs.at[s]).wait()
+            total = total + trb[s].astype(F32)
+        width = D // 8
+        at = pl.ds(pl.multiple_of(c * half_cols + me.x * width, width), width)
+        tfin[...] = (total * mt[2:3, at].astype(F32)).astype(BF16)
+        for share in shares:
+            share.start()
+        tall[me.x, half, c] = tfin[...]
+
+    relay(0)
+    for b in range(2):
+        for r in range(2):
+            @pl.when(jnp.logical_not(jnp.logical_and(home, jnp.logical_and(half == b, c == r))))
             def _():
-                pltpu.make_async_copy(trb.at[s], trb.at[s], trs.at[s]).wait()
-
-            @pl.when(s == mine)
-            def _():
-                trb[s] = tp[...]
-
-        total = trb[0].astype(F32)
-        for s in range(1, 8):
-            total = total + trb[s].astype(F32)
-        gate = mt[2:3, cols].astype(F32)
-        tfin[...] = (total * gate).astype(BF16)
-
-        def out(k, _):
-            piece_copy(k).start()
-            return 0
-
-        lax.fori_loop(1, 32, out, 0)
-        tpiece[lax.rem(level, 2), c] = tfin[...]
-
-    relay(0)
+                dst = tall.at[me.x, b, r]
+                pltpu.make_async_copy(dst, dst, br.at[b, r]).wait()
+
+    spreads = [
+        remote(tall.at[me.x], tall.at[me.x], xs.at[d], xr.at[d], device)
+        for d, device in enumerate(across)
+    ]
+    for copy in spreads:
+        copy.start()
     summed = collect(0)
     mirror.wait_recv()
     summed = summed + zb[...].astype(F32)
     video_out[...] = (summed * mv[2:3].astype(F32)).astype(BF16)
 
-    for b in range(2):
-        for r in range(2):
-            @pl.when(jnp.logical_not(jnp.logical_and(home, jnp.logical_and(lax.rem(level, 2) == b, c == r))))
-            def _():
-                pltpu.make_async_copy(tpiece.at[b, r], tpiece.at[b, r], br.at[b, r]).wait()
-            text_out[b * TXT : (b + 1) * TXT, r * half_cols : (r + 1) * half_cols] = tpiece[b, r]
+    for copy in spreads:
+        copy.wait_recv()
+    for k in range(4):
+        for b in range(2):
+            for r in range(2):
+                at = r * half_cols + k * (D // 8)
+                text_out[b * TXT : (b + 1) * TXT, at : at + D // 8] = tall[k, b, r]
     for p in (0, 1):
         far_copy(p).wait_send()
         plain_copy(p).wait_send()
         sum_copy(p).wait_send()
     mirror.wait_send()
 
-    @pl.when(jnp.logical_not(home))
-    def _():
-        gather_text.wait_send()
+    @pl.when(jnp.logical_not(own_piece))
+    def _():
+        text_parts[0].wait_send()
+
+    for copy in text_parts[1:] + spreads:
+        copy.wait_send()
 
     @pl.when(home)
     def _():
-        def done(k, _):
-            piece_copy(k).wait_send()
-            return 0
-
-        lax.fori_loop(1, 32, done, 0)
+        for share in shares:
+            share.wait_send()
 
 
 def finish(heads, theads, mv, mt, wv, wt):
@@ -638,14 +679,14 @@
             pltpu.VMEM((2, 2, CHUNK, D), BF16),
             pltpu.VMEM((CHUNK, D), BF16),
             pltpu.VMEM((CHUNK, D), BF16),
-            pltpu.VMEM((TXT, half_cols), BF16),
-            pltpu.VMEM((8, TXT, half_cols), BF16),
-            pltpu.VMEM((TXT, half_cols), BF16),
-            pltpu.VMEM((2, 2, TXT, half_cols), BF16),
+            pltpu.VMEM((4, TXT, D // 8), BF16),
+            pltpu.VMEM((8, TXT, D // 8), BF16),
+            pltpu.VMEM((TXT, D // 8), BF16),
+            pltpu.VMEM((4, 2, 2, TXT, D // 8), BF16),
             pltpu.VMEM((2 * HD, D), BF16),
             pltpu.VMEM((2 * HD, half_cols), BF16),
             DMA((2,)), DMA((2,)), DMA((2,)), DMA((2, 2)), DMA((2, 2)), DMA, DMA,
-            DMA((1,)), DMA((8,)), DMA((31,)), DMA((2, 2)),
+            DMA((4,)), DMA((8,)), DMA((7,)), DMA((2, 2)), DMA((3,)), DMA((3,)),
         ],
         compiler_params=pltpu.CompilerParams(collective_id=2, has_side_effects=True),
         name="finish",

time: 183 us -> 137 us (0.75)
  Pallas kernels: 177 us -> 133 us
    pallas_call x1, Pallas kernels: 77.9 us -> 52.3 us  [attend(): pl.pallas_call(attend_kernel, out_shape=(jax.ShapeDtypeStruct((ROWS, 2 *...]
    pallas_call x1, Pallas kernels: 59.3 us -> 42.6 us  [finish(): pl.pallas_call(finish_kernel, out_shape=(jax.ShapeDtypeStruct((CHUNK, D),...]
    pallas_call x1, Pallas kernels: 40.2 us -> 37.8 us  [project(): pl.pallas_call(project_kernel, out_shape=(jax.ShapeDtypeStruct((2, 3, ROW...]
where the time goes in v2:
time: 137 us
  Pallas kernels  133 us (97%)
  local copies, waits for them, and re-layouts  3.31 us (2%)
    pallas_call x1, Pallas kernels, attend(): pl.pallas_call(attend_kernel, out_shape=(jax.ShapeDtypeStruct((ROWS, 2 *...  52.3 us
    pallas_call x1, Pallas kernels, finish(): pl.pallas_call(finish_kernel, out_shape=(jax.ShapeDtypeStruct((CHUNK, D),...  42.6 us
    pallas_call x1, Pallas kernels, project(): pl.pallas_call(project_kernel, out_shape=(jax.ShapeDtypeStruct((2, 3, ROW...  37.8 us
    unnamed x2, local copies, waits for them, and re-layouts  3.31 us

profile of v2, /device:TPU:1, one launch (start us, length us, event | category | flops | bytes accessed | tf_op | source)
XLA Modules:
  0.0 136.6 jit_solution(8091948263931042365)
XLA Ops:
  0.6 37.8 %project.1 = (bf16[2,3,384,128]{3,2,1,0:T(8,128)(2,1)}, bf16[3,16,128]{2,1,0:T(8,128)(2,1)}) custom-call(bf16[48,3072]{1,0:T(8,128)(2,1)} %xv.1, bf16[32,3072]{1,0:T(8,128)(2,1)} %xt.1, bf16[3,3072]{1,0:T(4,128)(2,1)} %mv.3, bf16[3,3072]{1,0:T(4,128)(2,1)} %mt.3, f32[2,128]{1,0:T(2,128)} %gv.1, f32[2,128]{1,0:T(2,128)} %gt.1, bf16[3,3072,256]{2,1,0:T(8,128)(2,1)} %bitcast.2, ...), custom_call_target="tpu_custom_call" | custom-call | tf_op jit(solution)/shard_map/project/pallas_call | solution.py:212
  38.4 52.3 %attend.1 = (bf16[384,256]{1,0:T(8,128)(2,1)}, bf16[16,256]{1,0:T(8,128)(2,1)}) custom-call(bf16[2,3,384,128]{3,2,1,0:T(8,128)(2,1)} %get-tuple-element.6.qkv, bf16[3,16,128]{2,1,0:T(8,128)(2,1)} %get-tuple-element.7.tqkv), custom_call_target="tpu_custom_call" | custom-call | tf_op jit(solution)/shard_map/attend/pallas_call | solution.py:469
  90.7 42.6 %finish.1 = (bf16[48,3072]{1,0:T(8,128)(2,1)}, bf16[32,3072]{1,0:T(8,128)(2,1)}) custom-call(bf16[384,256]{1,0:T(8,128)(2,1)} %get-tuple-element.8.heads, bf16[16,256]{1,0:T(8,128)(2,1)} %get-tuple-element.9.theads, bf16[3,3072]{1,0:T(4,128)(2,1)} %mv.3, bf16[3,3072]{1,0:T(4,128)(2,1)} %mt.3, bf16[256,3072]{1,0:T(8,128)(2,1)} %wv_hbm.1, bf16[256,3072]{1,0:T(8,128)(2,1)} %wt_hbm.1), custom_call_target="tpu_custom_call" | custom-call | tf_op jit(solution)/shard_map/finish/pallas_call | solution.py:668
  133.3 1.7 %copy.14 = bf16[48,3072]{1,0:T(8,128)(2,1)} copy(bf16[48,3072]{1,0:T(8,128)(2,1)} %get-tuple-element.12) | data formatting | bytes 589824
  135.0 1.6 %copy.15 = bf16[32,3072]{1,0:T(8,128)(2,1)} copy(bf16[32,3072]{1,0:T(8,128)(2,1)} %get-tuple-element.13) | data formatting | bytes 393216

commit v3 on v2

v3 whole, which is shorter than its diff:
```python
import math

import jax
import jax.numpy as jnp
from jax import lax
from jax.experimental import pallas as pl
from jax.experimental.pallas import tpu as pltpu
from jax.sharding import Mesh
from jax.sharding import PartitionSpec as P

D = 3072
HD = 128
EPS = 1e-06
MESH = pl.DeviceIdType.MESH
AX = ("x", "zl", "c", "y", "zh")
ULY = ("y", "zh")
CHUNK = 48
ROWS = 8 * CHUNK
TXT = 16
LOG2 = math.log2(math.e) / math.sqrt(HD)
F32 = jnp.float32
BF16 = jnp.bfloat16


class Place:
    def __init__(self):
        self.x, self.zl, self.c, self.y, self.zh = (lax.axis_index(a) for a in AX)

    def at(self, **moved):
        found = {"x": self.x, "zl": self.zl, "c": self.c, "y": self.y, "zh": self.zh}
        found.update(moved)
        return found

    def group(self, dy, dz):
        y = lax.rem(self.y + dy, 4)
        if dz:
            return self.at(y=y, zh=1 - self.zh, zl=3 - self.zl)
        return self.at(y=y)

    def piece(self):
        return lax.rem(self.y + self.x, 4), jnp.where(self.zl < 2, self.zh, 1 - self.zh), lax.rem(self.zl, 2)


GROUP = [(dy, dz) for dz in (0, 1) for dy in range(4) if (dy, dz) != (0, 0)]


def greet(devices, more=0):
    barrier = pltpu.get_barrier_semaphore()
    for device in devices:
        pl.semaphore_signal(barrier, inc=1, device_id=device, device_id_type=MESH)
    return lambda: pl.semaphore_wait(barrier, len(devices) + more)


def remote(src, dst, ssem, rsem, device):
    return pltpu.make_async_remote_copy(
        src_ref=src, dst_ref=dst, send_sem=ssem, recv_sem=rsem,
        device_id=device, device_id_type=MESH,
    )


def modulate(rows, factors):
    floats = rows.astype(F32)
    centre = floats - jnp.mean(floats, axis=-1, keepdims=True)
    spread = jnp.mean(centre * centre, axis=-1, keepdims=True)
    normed = centre / jnp.sqrt(spread + EPS)
    return (normed * (1.0 + factors[1:2].astype(F32)) + factors[0:1].astype(F32)).astype(BF16)


def head_norm(vectors, gain):
    inverse = lax.rsqrt(jnp.mean(vectors * vectors, axis=-1, keepdims=True) + EPS)
    return (vectors * inverse * gain).astype(BF16)


HALF = ROWS // 2
SLOT = 2 * HALF
SPAN = 4 * SLOT


def mix_kernel(
    xv, xt, mv, mt, gv, gt, wv_hbm, wt_hbm, heads, theads,
    rows, ttmp, trow, wv, wt, qkv, tqkv, qb, kva, kvb, tq, mb, lb, ab,
    ob, sb, tob, orecv, srecv, trecv,
    wsem, gs, gr, tgs, tgr,
    kvs, kvr, qs, qr, tks, tkr, tqs, tqr, os_, or_, ss, sr, ts, tr,
):
    me = Place()
    c = me.c
    other = 1 - c
    load_v = pltpu.make_async_copy(wv_hbm, wv, wsem.at[0])
    load_t = pltpu.make_async_copy(
        wt_hbm.at[:, :, pl.ds(pl.multiple_of(c * HD, HD), HD)], wt, wsem.at[1]
    )
    load_v.start()
    load_t.start()
    peers = [me.group(dy, dz) for dy, dz in GROUP] + [me.at(c=other)]
    for d in range(1, 4):
        for r in (c, other):
            peers.append(me.at(x=lax.rem(me.x + d, 4), c=r))
            peers.append(me.at(zl=lax.rem(me.zl + d, 4), c=r))
    arrived = greet(peers)
    rows[0] = modulate(xv[...], mv[...])
    low_chip = me.zl < 2
    stays = jnp.logical_and(low_chip, me.x == 0)

    @pl.when(low_chip)
    def _():
        for b in range(2):
            ttmp[b] = modulate(xt[b * TXT : (b + 1) * TXT, :], mt[...])

    @pl.when(stays)
    def _():
        trow[...] = ttmp[me.zl]

    arrived()


    def copy_rows(src, dst, device):
        return remote(rows.at[src], rows.at[dst], gs.at[dst], gr.at[dst], device)

    up, down = me.group(1, 0), me.group(3, 0)
    far_src = 3 - 2 * c
    far_device = me.at(y=lax.rem(me.y + 1 + 2 * c, 4))

    mirror = copy_rows(0, 4, me.group(0, 1))
    mirror.start()

    def spread(base):
        low, high = copy_rows(base, base + 1, down), copy_rows(base, base + 3, up)

        @pl.when(c == 0)
        def _():
            high.start()
            low.start()

        @pl.when(c == 1)
        def _():
            low.start()
            high.start()

        return low, high

    def onward(base, low, high):
        far = copy_rows(base + far_src, base + 2, far_device)

        @pl.when(c == 0)
        def _():
            high.wait_recv()
            far.start()
            low.wait_recv()

        @pl.when(c == 1)
        def _():
            low.wait_recv()
            far.start()
            high.wait_recv()

        return far

    text_y = lax.rem(me.y + 4 - me.x, 4)
    text_near = remote(ttmp.at[lax.rem(me.zl, 2)], trow, tgs.at[0], tgr, me.at(y=text_y))
    text_over = remote(
        ttmp.at[1 - lax.rem(me.zl, 2)], trow, tgs.at[1], tgr,
        me.at(y=text_y, zh=1 - me.zh, zl=3 - me.zl),
    )

    def block(p):
        lhs = rows[4 * p : 4 * p + 4].reshape(HALF, D)
        for j in range(3):
            total = jnp.dot(lhs, wv[j], preferred_element_type=F32)
            for h in range(2):
                part = total[:, h * HD : (h + 1) * HD]
                part = head_norm(part, gv[j : j + 1]) if j < 2 else part.astype(BF16)
                qkv[h, p, j] = part


    sends = []

    def send(copy):
        copy.start()
        sends.append(copy)

    def kv_rows(p, slot, core):
        at = pl.ds(pl.multiple_of(slot * SLOT + core * HALF, HALF), HALF)
        return (kvb if p else kva).at[:, at, :]

    def q_rows(p, slot, core):
        return qb.at[p, slot, pl.ds(pl.multiple_of(core * HALF, HALF), HALF), :]

    def kv_text(slot):
        return kvb.at[:, pl.ds(SPAN + TXT * slot, TXT), :]

    def q_text(slot):
        return tq.at[pl.ds(TXT * slot, TXT), :]

    def along(axis, d, r):
        return me.at(**{axis: lax.rem(getattr(me, axis) + d, 4), "c": r})

    def exchange(p):
        pltpu.make_async_copy(qkv.at[c, p, 0], q_rows(p, 0, c), qr.at[p, 0, 0]).start()
        pltpu.make_async_copy(
            qkv.at[c, p, pl.ds(1, 2)], kv_rows(p, 0, c), kvr.at[p, 0, 0]
        ).start()
        for d in (0, 3, 1, 2):
            slot = (4 - d) % 4
            for i, r in enumerate((c, other)):
                if d or i:
                    send(remote(
                        qkv.at[r, p, 0], q_rows(p, slot, c),
                        qs.at[p, slot, i], qr.at[p, slot, i], along("zl", d, r),
                    ))
            for i, r in enumerate((c, other)):
                if d or i:
                    send(remote(
                        qkv.at[r, p, pl.ds(1, 2)], kv_rows(p, slot, c),
                        kvs.at[p, slot, i], kvr.at[p, slot, i], along("x", d, r),
                    ))

    def exchange_text():
        pltpu.make_async_copy(tqkv.at[0], q_text(0), tqr.at[0]).start()
        pltpu.make_async_copy(tqkv.at[pl.ds(1, 2)], kv_text(0), tkr.at[0]).start()
        for d in (3, 1, 2):
            slot = (4 - d) % 4
            send(remote(tqkv.at[0], q_text(slot), tqs.at[slot], tqr.at[slot], along("zl", d, c)))
            send(remote(
                tqkv.at[pl.ds(1, 2)], kv_text(slot), tks.at[slot], tkr.at[slot], along("x", d, c)
            ))

    def landed(dst, sem):
        pltpu.make_async_copy(dst, dst, sem).wait()

    def await_kv(p):
        for slot in (0, 1, 3, 2):
            for i in range(2):
                landed(kv_rows(p, slot, i), kvr.at[p, slot, i])

    def await_q(p, slot):
        for i in range(2):
            landed(q_rows(p, slot, i), qr.at[p, slot, i])

    def scored(queries, keys):
        return lax.dot_general(
            queries, keys, (((1,), (1,)), ((), ())), preferred_element_type=F32
        )

    def lanes(weights):
        width = weights.shape[1]
        if width % HD:
            extra = weights[:, width - width % HD :]
            pad = jnp.zeros((extra.shape[0], HD - width % HD), F32)
            total = jnp.concatenate([extra, pad], axis=1)
        else:
            total = jnp.zeros((weights.shape[0], HD), F32)
        for k in range(width // HD):
            total = total + weights[:, k * HD : (k + 1) * HD]
        return total

    def open_step(queries, at):
        scores = scored(queries, kva[0])
        now = jnp.max(scores, axis=-1, keepdims=True)
        weights = jnp.exp2((scores - now) * LOG2)
        mb[at, :] = jnp.broadcast_to(now, (queries.shape[0], HD))
        lb[at, :] = lanes(weights)
        ab[at, :] = jnp.dot(weights.astype(BF16), kva[1], preferred_element_type=F32)

    def last_step(queries, at):
        scores = scored(queries, kvb[0])
        before = mb[at, :]
        now = jnp.maximum(before[:, :1], jnp.max(scores, axis=-1, keepdims=True))
        weights = jnp.exp2((scores - now) * LOG2)
        shrink = jnp.exp2((before - now) * LOG2)
        totals = jnp.sum(lb[at, :] * shrink + lanes(weights), axis=-1, keepdims=True)
        sums = ab[at, :] * shrink + jnp.dot(
            weights.astype(BF16), kvb[1], preferred_element_type=F32
        )
        level = jnp.broadcast_to(now * LOG2 + jnp.log2(totals), sums.shape)
        return sums / totals, level

    tail = pl.ds(2 * SPAN, 4 * TXT)

    def state_rows(p, slot):
        return pl.ds(pl.multiple_of((p * 4 + slot) * SLOT, SLOT), SLOT)

    def open_phase(p):
        def pair(i, _):
            slots = (3 * i, 1 + i)
            for slot in slots:
                await_q(p, slot)
            for slot in slots:
                open_step(qb[p, slot], state_rows(p, slot))
            return 0

        lax.fori_loop(0, 2, pair, 0)

    def out_copies(p, j, slot, i, r):
        device = along("zl", j, r)
        return (
            remote(
                ob.at[p, j, pl.ds(pl.multiple_of(r * HALF, HALF), HALF), :], orecv.at[p, slot, c],
                os_.at[p, slot, i], or_.at[p, slot, i], device,
            ),
            remote(
                sb.at[p, j, r], srecv.at[p, slot, c], ss.at[p, slot, i], sr.at[p, slot, i], device
            ),
        )

    def last_phase(p):
        def pair(n, _):
            slots = (2 - 2 * n, 3 - 2 * n)
            for slot in slots:
                mixed, level = last_step(qb[p, slot], state_rows(p, slot))
                ob[p, slot] = mixed.astype(BF16)
                for r in range(2):
                    part = level[r * HALF : (r + 1) * HALF]
                    sb[p, slot, r] = jnp.transpose(part)[:8, :]

            @pl.when(n == 0)
            def _():
                for j in (2, 3):
                    for i, r in enumerate((c, other)):
                        for copy in out_copies(p, j, 4 - j, i, r):
                            copy.start()

            @pl.when(n == 1)
            def _():
                for i, r in enumerate((c, other)):
                    for copy in out_copies(p, 1, 3, i, r):
                        copy.start()
                for copy in out_copies(p, 0, 0, 1, other):
                    copy.start()
                at = pl.ds(pl.multiple_of(c * HALF, HALF), HALF)
                pltpu.make_async_copy(
                    ob.at[p, 0, at, :], orecv.at[p, 0, c], or_.at[p, 0, 0]
                ).start()
                pltpu.make_async_copy(sb.at[p, 0, c], srecv.at[p, 0, c], sr.at[p, 0, 0]).start()

            return 0

        lax.fori_loop(0, 2, pair, 0)

    def merge(p):
        for slot in range(4):
            for i, r in enumerate((c, other)):
                landed(orecv.at[p, slot, r], or_.at[p, slot, i])
                landed(srecv.at[p, slot, r], sr.at[p, slot, i])
        for h in range(2):
            found = [srecv[p, slot, h] for slot in range(4)]
            top = jnp.maximum(jnp.maximum(found[0], found[1]), jnp.maximum(found[2], found[3]))
            weight = [jnp.exp2(part - top) for part in found]
            share = 1.0 / sum(weight)
            mixed = jnp.zeros((HALF, HD), F32)
            for slot in range(4):
                row = (weight[slot] * share)[:1]
                column = jnp.transpose(jnp.broadcast_to(row, (HD, HALF)))
                mixed = mixed + column * orecv[p, slot, h].astype(F32)
            heads[p * HALF : (p + 1) * HALF, h * HD : (h + 1) * HD] = mixed.astype(BF16)

    def send_text():
        mixed, level = last_step(tq[...], tail)
        tob[:, :HD] = mixed
        tob[:, HD:] = level
        for j in range(4):
            slot = (4 - j) % 4
            for i, r in enumerate((c, other)):
                src, dst = tob.at[pl.ds(TXT * j, TXT), :], trecv.at[slot, c]
                if j == 0 and i == 0:
                    pltpu.make_async_copy(src, dst, tr.at[0, 0]).start()
                else:
                    send(remote(src, dst, ts.at[slot, i], tr.at[slot, i], along("zl", j, r)))

    def merge_text():
        for slot in range(4):
            for i, r in enumerate((c, other)):
                landed(trecv.at[slot, r], tr.at[slot, i])
        for h in range(2):
            found = [trecv[slot, h] for slot in range(4)]
            top = found[0][:, HD:]
            for part in found[1:]:
                top = jnp.maximum(top, part[:, HD:])
            weight = [jnp.exp2(part[:, HD:] - top) for part in found]
            mixed = sum(w * part[:, :HD] for w, part in zip(weight, found)) / sum(weight)
            theads[:, h * HD : (h + 1) * HD] = mixed.astype(BF16)

    first = spread(0)

    @pl.when(low_chip)
    def _():
        text_over.start()

    @pl.when(jnp.logical_and(low_chip, me.x > 0))
    def _():
        text_near.start()

    far0 = onward(0, *first)
    mirror.wait_recv()
    second = spread(4)
    load_v.wait()
    far0.wait_recv()
    block(0)
    exchange(0)
    far1 = onward(4, *second)

    @pl.when(jnp.logical_not(stays))
    def _():
        text_near.wait_recv()

    load_t.wait()
    for j in range(3):
        part = jnp.dot(trow[...], wt[j], preferred_element_type=F32)
        tqkv[j] = head_norm(part, gt[j : j + 1]) if j < 2 else part.astype(BF16)
    exchange_text()
    await_kv(0)
    open_phase(0)
    far1.wait_recv()
    block(1)
    exchange(1)
    for j in range(4):
        landed(q_text(j), tqr.at[j])
    open_step(tq[...], tail)
    open_phase(1)
    await_kv(1)
    for j in range(4):
        landed(kv_text(j), tkr.at[j])
    send_text()
    last_phase(1)
    last_phase(0)
    merge_text()
    merge(1)
    merge(0)

    for copy in (mirror, *first, far0, *second, far1):
        copy.wait_send()

    @pl.when(low_chip)
    def _():
        text_over.wait_send()

    @pl.when(jnp.logical_and(low_chip, me.x > 0))
    def _():
        text_near.wait_send()

    for copy in sends:
        copy.wait_send()
    for p in range(2):
        for slot in range(4):
            for i, r in enumerate((c, other)):
                if (slot, i) != (0, 0):
                    for copy in out_copies(p, (4 - slot) % 4, slot, i, r):
                        copy.wait_send()


def vmem(n):
    return [pl.BlockSpec(memory_space=pltpu.VMEM)] * n


def hbm(n):
    return [pl.BlockSpec(memory_space=pl.ANY)] * n


DMA = pltpu.SemaphoreType.DMA


def mix(xv, xt, mv, mt, gv, gt, wv, wt):
    states = 2 * SPAN + 4 * TXT
    return pl.pallas_call(
        mix_kernel,
        out_shape=(
            jax.ShapeDtypeStruct((ROWS, 2 * HD), BF16),
            jax.ShapeDtypeStruct((TXT, 2 * HD), BF16),
        ),
        in_specs=vmem(6) + hbm(2),
        out_specs=tuple(vmem(2)),
        scratch_shapes=[
            pltpu.VMEM((8, CHUNK, D), BF16),
            pltpu.VMEM((2, TXT, D), BF16),
            pltpu.VMEM((TXT, D), BF16),
            pltpu.VMEM((3, D, 2 * HD), BF16),
            pltpu.VMEM((3, D, HD), BF16),
            pltpu.VMEM((2, 2, 3, HALF, HD), BF16),
            pltpu.VMEM((3, TXT, HD), BF16),
            pltpu.VMEM((2, 4, SLOT, HD), BF16),
            pltpu.VMEM((2, SPAN, HD), BF16),
            pltpu.VMEM((2, SPAN + 4 * TXT, HD), BF16),
            pltpu.VMEM((4 * TXT, HD), BF16),
            pltpu.VMEM((states, HD), F32),
            pltpu.VMEM((states, HD), F32),
            pltpu.VMEM((states, HD), F32),
            pltpu.VMEM((2, 4, SLOT, HD), BF16),
            pltpu.VMEM((2, 4, 2, 8, HALF), F32),
            pltpu.VMEM((4 * TXT, 2 * HD), F32),
            pltpu.VMEM((2, 4, 2, HALF, HD), BF16),
            pltpu.VMEM((2, 4, 2, 8, HALF), F32),
            pltpu.VMEM((4, 2, TXT, 2 * HD), F32),
            DMA((2,)), DMA((8,)), DMA((8,)), DMA((2,)), DMA,
        ]
        + [DMA((2, 4, 2))] * 4 + [DMA((4,))] * 4 + [DMA((2, 4, 2))] * 4 + [DMA((4, 2))] * 2,
        compiler_params=pltpu.CompilerParams(collective_id=0, has_side_effects=True),
        name="mix",
    )(xv, xt, mv, mt, gv, gt, wv, wt)


def finish_kernel(
    heads, theads, mv, mt, wv_hbm, wt_hbm, video_out, text_out,
    pb, fb, nb, zb, zs, tp, trb, tfin, tall, wv, wt,
    wsem, fs, fr, ns, nr, zsem, zr, tss, trs, bs, br, xs, xr,
):
    me = Place()
    c = me.c
    half_cols = D // 2
    load_v = pltpu.make_async_copy(wv_hbm, wv, wsem.at[0])
    cols = pl.ds(pl.multiple_of(c * half_cols, half_cols), half_cols)
    load_t = pltpu.make_async_copy(wt_hbm.at[:, cols], wt, wsem.at[1])
    load_v.start()
    load_t.start()
    piece_y, piece_zh, half = me.piece()
    mine = me.y * 2 + me.zh
    home = me.zl // 2 == c

    def gatherer(k):
        return me.at(x=k, zl=2 * c + half, y=piece_y, zh=piece_zh)

    def giver(s):
        y, zh = s // 2, s % 2
        side = jnp.where(me.zh == zh, 0, 1)
        return me.at(x=lax.rem(me.y + 4 - y, 4), zl=2 * side + half, y=y, zh=zh)

    own_piece = jnp.logical_and(me.x == 0, jnp.logical_and(me.zl < 2, c == 0))
    column = [me.at(zl=lax.rem(me.zl + d, 4), c=r) for d in range(4) for r in (c, 1 - c)]
    across = [me.at(x=lax.rem(me.x + d, 4)) for d in range(1, 4)]
    up, down = me.group(1, 0), me.group(3, 0)
    arrived = greet(
        [up, down, me.group(0, 1)] + column[1:] + across,
        4 - jnp.where(own_piece, 1, 0),
    )
    barrier = pltpu.get_barrier_semaphore()

    @pl.when(home)
    def _():
        for s in range(8):
            @pl.when(jnp.logical_not(jnp.logical_and(own_piece, s == mine)))
            def _():
                pl.semaphore_signal(barrier, inc=1, device_id=giver(s), device_id_type=MESH)

    load_t.wait()
    part = jnp.dot(theads[...], wt[...], preferred_element_type=F32).astype(BF16)
    for k in range(4):
        tp[k] = part[:, k * (D // 8) : (k + 1) * (D // 8)]
    load_v.wait()
    for p in (1, 0):
        lhs = heads[p * 4 * CHUNK : (p + 1) * 4 * CHUNK, :]
        for q in range(4):
            span = slice(q * (D // 4), (q + 1) * (D // 4))
            found = jnp.dot(lhs, wv[:, span], preferred_element_type=F32).astype(BF16)
            pb[4 * p : 4 * p + 4, :, span] = found.reshape(4, CHUNK, D // 4)
    arrived()

    text_parts = [
        remote(tp.at[k], trb.at[mine], tss.at[k], trs.at[mine], gatherer(k)) for k in range(4)
    ]
    own_part = pltpu.make_async_copy(tp.at[0], trb.at[mine], trs.at[mine])

    @pl.when(own_piece)
    def _():
        own_part.start()

    @pl.when(jnp.logical_not(own_piece))
    def _():
        text_parts[0].start()

    for text_part in text_parts[1:]:
        text_part.start()
    far_device = me.at(y=lax.rem(me.y + 3 + 2 * c, 4))
    near_device = far_device
    near_slot = 3 - 2 * c
    plain_device = me.at(y=lax.rem(me.y + 1 + 2 * c, 4))
    plain_slot = 1 + 2 * c

    def far_copy(p):
        return remote(pb.at[4 * p + 2], fb.at[p], fs.at[p], fr.at[p], far_device)

    def plain_copy(p):
        return remote(pb.at[4 * p + plain_slot], nb.at[p, 0], ns.at[p, 0], nr.at[p, 0], plain_device)

    def sum_copy(p):
        return remote(pb.at[4 * p + near_slot], nb.at[p, 1], ns.at[p, 1], nr.at[p, 1], near_device)

    for p in (1, 0):
        far_copy(p).start()
        plain_copy(p).start()

    def relay(p):
        far_copy(p).wait_recv()
        total = pb[4 * p + near_slot].astype(F32) + fb[p].astype(F32)
        pb[4 * p + near_slot] = total.astype(BF16)
        sum_copy(p).start()

    def collect(p):
        plain_copy(p).wait_recv()
        sum_copy(p).wait_recv()
        return pb[4 * p].astype(F32) + nb[p, 0].astype(F32) + nb[p, 1].astype(F32)

    mirror = remote(zs, zb, zsem, zr, me.group(0, 1))
    relay(1)
    zs[...] = collect(1).astype(BF16)
    mirror.start()

    shares = [
        remote(tfin, tall.at[me.x, half, c], bs.at[i], br.at[half, c], device)
        for i, device in enumerate(column[1:])
    ]

    @pl.when(home)
    def _():
        total = jnp.zeros((TXT, D // 8), F32)
        for s in range(8):
            pltpu.make_async_copy(trb.at[s], trb.at[s], trs.at[s]).wait()
            total = total + trb[s].astype(F32)
        width = D // 8
        at = pl.ds(pl.multiple_of(c * half_cols + me.x * width, width), width)
        tfin[...] = (total * mt[2:3, at].astype(F32)).astype(BF16)
        for share in shares:
            share.start()
        tall[me.x, half, c] = tfin[...]

    relay(0)
    for b in range(2):
        for r in range(2):
            @pl.when(jnp.logical_not(jnp.logical_and(home, jnp.logical_and(half == b, c == r))))
            def _():
                dst = tall.at[me.x, b, r]
                pltpu.make_async_copy(dst, dst, br.at[b, r]).wait()

    spreads = [
        remote(tall.at[me.x], tall.at[me.x], xs.at[d], xr.at[d], device)
        for d, device in enumerate(across)
    ]
    for copy in spreads:
        copy.start()
    summed = collect(0)
    mirror.wait_recv()
    summed = summed + zb[...].astype(F32)
    video_out[...] = (summed * mv[2:3].astype(F32)).astype(BF16)

    for copy in spreads:
        copy.wait_recv()
    for k in range(4):
        for b in range(2):
            for r in range(2):
                at = r * half_cols + k * (D // 8)
                text_out[b * TXT : (b + 1) * TXT, at : at + D // 8] = tall[k, b, r]
    for p in (0, 1):
        far_copy(p).wait_send()
        plain_copy(p).wait_send()
        sum_copy(p).wait_send()
    mirror.wait_send()

    @pl.when(jnp.logical_not(own_piece))
    def _():
        text_parts[0].wait_send()

    for copy in text_parts[1:] + spreads:
        copy.wait_send()

    @pl.when(home)
    def _():
        for share in shares:
            share.wait_send()


def finish(heads, theads, mv, mt, wv, wt):
    half_cols = D // 2
    return pl.pallas_call(
        finish_kernel,
        out_shape=(
            jax.ShapeDtypeStruct((CHUNK, D), BF16),
            jax.ShapeDtypeStruct((2 * TXT, D), BF16),
        ),
        in_specs=vmem(4) + hbm(2),
        out_specs=tuple(vmem(2)),
        scratch_shapes=[
            pltpu.VMEM((8, CHUNK, D), BF16),
            pltpu.VMEM((2, CHUNK, D), BF16),
            pltpu.VMEM((2, 2, CHUNK, D), BF16),
            pltpu.VMEM((CHUNK, D), BF16),
            pltpu.VMEM((CHUNK, D), BF16),
            pltpu.VMEM((4, TXT, D // 8), BF16),
            pltpu.VMEM((8, TXT, D // 8), BF16),
            pltpu.VMEM((TXT, D // 8), BF16),
            pltpu.VMEM((4, 2, 2, TXT, D // 8), BF16),
            pltpu.VMEM((2 * HD, D), BF16),
            pltpu.VMEM((2 * HD, half_cols), BF16),
            DMA((2,)), DMA((2,)), DMA((2,)), DMA((2, 2)), DMA((2, 2)), DMA, DMA,
            DMA((4,)), DMA((8,)), DMA((7,)), DMA((2, 2)), DMA((3,)), DMA((3,)),
        ],
        compiler_params=pltpu.CompilerParams(collective_id=1, has_side_effects=True),
        name="finish",
    )(heads, theads, mv, mt, wv, wt)


def local(
    video_tokens, text_tokens, video_modulation, text_modulation, video_projection,
    text_projection, video_output, text_output, video_gains, text_gains,
):
    heads, theads = mix(
        video_tokens, text_tokens, video_modulation, text_modulation, video_gains, text_gains,
        jnp.transpose(video_projection, (1, 0, 2)), jnp.transpose(text_projection, (1, 0, 2)),
    )
    return finish(heads, theads, video_modulation, text_modulation, video_output, text_output)


def solution(mesh):
    torus = Mesh(mesh.devices.reshape(4, 4, 2, 4, 2), AX)
    placed = (
        P(AX, None),
        P(ULY, None),
        P(),
        P(),
        P(None, None, ULY),
        P(None, None, ULY),
        P(ULY, None),
        P(ULY, None),
        P(),
        P(),
    )
    return jax.shard_map(
        local,
        mesh=torus,
        in_specs=placed,
        out_specs=(P(AX, None), P(ULY, None)),
        check_vma=False,
    )
```

time: 137 us -> 130 us (0.949)
  Pallas kernels: 133 us -> 125 us
    pallas_call x2 -> x1, Pallas kernels: 90.1 us -> 83.1 us  [mix(): pl.pallas_call(mix_kernel, out_shape=(jax.ShapeDtypeStruct((ROWS, 2 * HD)...]
where the time goes in v3:
time: 130 us; the launch traced here: 129 us
  Pallas kernels  125 us (96%)
  local copies, waits for them, and re-layouts  3.31 us (3%)
    pallas_call x1, Pallas kernels, mix(): pl.pallas_call(mix_kernel, out_shape=(jax.ShapeDtypeStruct((ROWS, 2 * HD)...  83.1 us
    pallas_call x1, Pallas kernels, finish(): pl.pallas_call(finish_kernel, out_shape=(jax.ShapeDtypeStruct((CHUNK, D),...  42.4 us
    unnamed x2, local copies, waits for them, and re-layouts  3.31 us

profile of v3, /device:TPU:1, one launch (start us, length us, event | category | flops | bytes accessed | tf_op | source)
XLA Modules:
  0.0 129.4 jit_solution(3445184996888839390)
XLA Ops:
  0.6 83.1 %mix.1 = (bf16[384,256]{1,0:T(8,128)(2,1)}, bf16[16,256]{1,0:T(8,128)(2,1)}) custom-call(bf16[48,3072]{1,0:T(8,128)(2,1)} %xv.1, bf16[32,3072]{1,0:T(8,128)(2,1)} %xt.1, bf16[3,3072]{1,0:T(4,128)(2,1)} %mv.3, bf16[3,3072]{1,0:T(4,128)(2,1)} %mt.3, f32[2,128]{1,0:T(2,128)} %gv.1, f32[2,128]{1,0:T(2,128)} %gt.1, bf16[3,3072,256]{2,1,0:T(8,128)(2,1)} %bitcast.2, ...), custom_call_target="tpu_custom_call" | custom-call | tf_op jit(solution)/shard_map/mix/pallas_call | solution.py:464
  83.7 42.4 %finish.1 = (bf16[48,3072]{1,0:T(8,128)(2,1)}, bf16[32,3072]{1,0:T(8,128)(2,1)}) custom-call(bf16[384,256]{1,0:T(8,128)(2,1)} %get-tuple-element.4.heads, bf16[16,256]{1,0:T(8,128)(2,1)} %get-tuple-element.5.theads, bf16[3,3072]{1,0:T(4,128)(2,1)} %mv.3, bf16[3,3072]{1,0:T(4,128)(2,1)} %mt.3, bf16[256,3072]{1,0:T(8,128)(2,1)} %wv_hbm.1, bf16[256,3072]{1,0:T(8,128)(2,1)} %wt_hbm.1), custom_call_target="tpu_custom_call" | custom-call | tf_op jit(solution)/shard_map/finish/pallas_call | solution.py:671
  126.1 1.7 %copy.14 = bf16[48,3072]{1,0:T(8,128)(2,1)} copy(bf16[48,3072]{1,0:T(8,128)(2,1)} %get-tuple-element.8) | data formatting | bytes 589824
  127.8 1.6 %copy.15 = bf16[32,3072]{1,0:T(8,128)(2,1)} copy(bf16[32,3072]{1,0:T(8,128)(2,1)} %get-tuple-element.9) | data formatting | bytes 393216

commit v4 on v3

--- a/solution.py
+++ b/solution.py
@@ -115,46 +115,56 @@
 
 
     def copy_rows(src, dst, device):
-        return remote(rows.at[src], rows.at[dst], gs.at[dst], gr.at[dst], device)
+        return [
+            remote(
+                rows.at[src, :, pl.ds(h * (D // 2), D // 2)], rows.at[dst, :, pl.ds(h * (D // 2), D // 2)],
+                gs.at[dst, h], gr.at[dst, h], device,
+            )
+            for h in range(2)
+        ]
 
     up, down = me.group(1, 0), me.group(3, 0)
     far_src = 3 - 2 * c
     far_device = me.at(y=lax.rem(me.y + 1 + 2 * c, 4))
-
     mirror = copy_rows(0, 4, me.group(0, 1))
-    mirror.start()
-
-    def spread(base):
-        low, high = copy_rows(base, base + 1, down), copy_rows(base, base + 3, up)
+    moves = [
+        (copy_rows(b, b + 1, down), copy_rows(b, b + 3, up), copy_rows(b + far_src, b + 2, far_device))
+        for b in (0, 4)
+    ]
+
+    def spread(p, h):
+        low, high, _ = moves[p]
+        high[h].start()
+        low[h].start()
+
+    def onward(p, h):
+        low, high, far = moves[p]
 
         @pl.when(c == 0)
         def _():
-            high.start()
-            low.start()
+            high[h].wait_recv()
 
         @pl.when(c == 1)
         def _():
-            low.start()
-            high.start()
-
-        return low, high
-
-    def onward(base, low, high):
-        far = copy_rows(base + far_src, base + 2, far_device)
+            low[h].wait_recv()
+
+        far[h].start()
+
+    def gathered(p):
+        low, high, far = moves[p]
 
         @pl.when(c == 0)
         def _():
-            high.wait_recv()
-            far.start()
-            low.wait_recv()
+            for copy in low:
+                copy.wait_recv()
 
         @pl.when(c == 1)
         def _():
-            low.wait_recv()
-            far.start()
-            high.wait_recv()
-
-        return far
+            for copy in high:
+                copy.wait_recv()
+
+        for copy in far:
+            copy.wait_recv()
 
     text_y = lax.rem(me.y + 4 - me.x, 4)
     text_near = remote(ttmp.at[lax.rem(me.zl, 2)], trow, tgs.at[0], tgr, me.at(y=text_y))
@@ -206,13 +216,13 @@
                 if d or i:
                     send(remote(
                         qkv.at[r, p, 0], q_rows(p, slot, c),
-                        qs.at[p, slot, i], qr.at[p, slot, i], along("zl", d, r),
+                        qs.at[p, slot, i], qr.at[p, slot, i], along("x", d, r),
                     ))
             for i, r in enumerate((c, other)):
                 if d or i:
                     send(remote(
                         qkv.at[r, p, pl.ds(1, 2)], kv_rows(p, slot, c),
-                        kvs.at[p, slot, i], kvr.at[p, slot, i], along("x", d, r),
+                        kvs.at[p, slot, i], kvr.at[p, slot, i], along("zl", d, r),
                     ))
 
     def exchange_text():
@@ -220,9 +230,9 @@
         pltpu.make_async_copy(tqkv.at[pl.ds(1, 2)], kv_text(0), tkr.at[0]).start()
         for d in (3, 1, 2):
             slot = (4 - d) % 4
-            send(remote(tqkv.at[0], q_text(slot), tqs.at[slot], tqr.at[slot], along("zl", d, c)))
+            send(remote(tqkv.at[0], q_text(slot), tqs.at[slot], tqr.at[slot], along("x", d, c)))
             send(remote(
-                tqkv.at[pl.ds(1, 2)], kv_text(slot), tks.at[slot], tkr.at[slot], along("x", d, c)
+                tqkv.at[pl.ds(1, 2)], kv_text(slot), tks.at[slot], tkr.at[slot], along("zl", d, c)
             ))
 
     def landed(dst, sem):
@@ -292,7 +302,7 @@
         lax.fori_loop(0, 2, pair, 0)
 
     def out_copies(p, j, slot, i, r):
-        device = along("zl", j, r)
+        device = along("x", j, r)
         return (
             remote(
                 ob.at[p, j, pl.ds(pl.multiple_of(r * HALF, HALF), HALF), :], orecv.at[p, slot, c],
@@ -365,7 +375,7 @@
                 if j == 0 and i == 0:
                     pltpu.make_async_copy(src, dst, tr.at[0, 0]).start()
                 else:
-                    send(remote(src, dst, ts.at[slot, i], tr.at[slot, i], along("zl", j, r)))
+                    send(remote(src, dst, ts.at[slot, i], tr.at[slot, i], along("x", j, r)))
 
     def merge_text():
         for slot in range(4):
@@ -380,7 +390,10 @@
             mixed = sum(w * part[:, :HD] for w, part in zip(weight, found)) / sum(weight)
             theads[:, h * HD : (h + 1) * HD] = mixed.astype(BF16)
 
-    first = spread(0)
+    mirror[0].start()
+    spread(0, 0)
+    mirror[1].start()
+    spread(0, 1)
 
     @pl.when(low_chip)
     def _():
@@ -390,14 +403,17 @@
     def _():
         text_near.start()
 
-    far0 = onward(0, *first)
-    mirror.wait_recv()
-    second = spread(4)
+    onward(0, 0)
+    onward(0, 1)
+    for h in range(2):
+        mirror[h].wait_recv()
+        spread(1, h)
     load_v.wait()
-    far0.wait_recv()
+    gathered(0)
     block(0)
     exchange(0)
-    far1 = onward(4, *second)
+    onward(1, 0)
+    onward(1, 1)
 
     @pl.when(jnp.logical_not(stays))
     def _():
@@ -410,7 +426,7 @@
     exchange_text()
     await_kv(0)
     open_phase(0)
-    far1.wait_recv()
+    gathered(1)
     block(1)
     exchange(1)
     for j in range(4):
@@ -427,8 +443,9 @@
     merge(1)
     merge(0)
 
-    for copy in (mirror, *first, far0, *second, far1):
-        copy.wait_send()
+    for pair in [mirror] + [found for move in moves for found in move]:
+        for copy in pair:
+            copy.wait_send()
 
     @pl.when(low_chip)
     def _():
@@ -490,7 +507,7 @@
             pltpu.VMEM((2, 4, 2, HALF, HD), BF16),
             pltpu.VMEM((2, 4, 2, 8, HALF), F32),
             pltpu.VMEM((4, 2, TXT, 2 * HD), F32),
-            DMA((2,)), DMA((8,)), DMA((8,)), DMA((2,)), DMA,
+            DMA((2,)), DMA((8, 2)), DMA((8, 2)), DMA((2,)), DMA,
         ]
         + [DMA((2, 4, 2))] * 4 + [DMA((4,))] * 4 + [DMA((2, 4, 2))] * 4 + [DMA((4, 2))] * 2,
         compiler_params=pltpu.CompilerParams(collective_id=0, has_side_effects=True),
@@ -545,14 +562,69 @@
     for k in range(4):
         tp[k] = part[:, k * (D // 8) : (k + 1) * (D // 8)]
     load_v.wait()
-    for p in (1, 0):
+
+    def block(p):
         lhs = heads[p * 4 * CHUNK : (p + 1) * 4 * CHUNK, :]
         for q in range(4):
             span = slice(q * (D // 4), (q + 1) * (D // 4))
             found = jnp.dot(lhs, wv[:, span], preferred_element_type=F32).astype(BF16)
             pb[4 * p : 4 * p + 4, :, span] = found.reshape(4, CHUNK, D // 4)
+
+    block(1)
     arrived()
 
+    far_device = me.at(y=lax.rem(me.y + 3 + 2 * c, 4))
+    near_slot = 3 - 2 * c
+    plain_device = me.at(y=lax.rem(me.y + 1 + 2 * c, 4))
+    plain_slot = 1 + 2 * c
+
+    def part_of(h):
+        return pl.ds(h * half_cols, half_cols)
+
+    def far_copy(p, h):
+        return remote(
+            pb.at[4 * p + 2, :, part_of(h)], fb.at[p, :, part_of(h)],
+            fs.at[p, h], fr.at[p, h], far_device,
+        )
+
+    def plain_copy(p, h):
+        return remote(
+            pb.at[4 * p + plain_slot, :, part_of(h)], nb.at[p, 0, :, part_of(h)],
+            ns.at[p, 0, h], nr.at[p, 0, h], plain_device,
+        )
+
+    def sum_copy(p, h):
+        return remote(
+            pb.at[4 * p + near_slot, :, part_of(h)], nb.at[p, 1, :, part_of(h)],
+            ns.at[p, 1, h], nr.at[p, 1, h], far_device,
+        )
+
+    def mirror_copy(h):
+        return remote(
+            zs.at[:, part_of(h)], zb.at[:, part_of(h)], zsem.at[h], zr.at[h], me.group(0, 1)
+        )
+
+    def depart(p):
+        for h in range(2):
+            far_copy(p, h).start()
+            plain_copy(p, h).start()
+
+    def relay(p, h):
+        far_copy(p, h).wait_recv()
+        at = part_of(h)
+        total = pb[4 * p + near_slot, :, at].astype(F32) + fb[p, :, at].astype(F32)
+        pb[4 * p + near_slot, :, at] = total.astype(BF16)
+        sum_copy(p, h).start()
+
+    def collect(p, h):
+        plain_copy(p, h).wait_recv()
+        sum_copy(p, h).wait_recv()
+        at = part_of(h)
+        return (
+            pb[4 * p, :, at].astype(F32) + nb[p, 0, :, at].astype(F32) + nb[p, 1, :, at].astype(F32)
+        )
+
+    depart(1)
     text_parts = [
         remote(tp.at[k], trb.at[mine], tss.at[k], trs.at[mine], gatherer(k)) for k in range(4)
     ]
@@ -568,40 +640,13 @@
 
     for text_part in text_parts[1:]:
         text_part.start()
-    far_device = me.at(y=lax.rem(me.y + 3 + 2 * c, 4))
-    near_device = far_device
-    near_slot = 3 - 2 * c
-    plain_device = me.at(y=lax.rem(me.y + 1 + 2 * c, 4))
-    plain_slot = 1 + 2 * c
-
-    def far_copy(p):
-        return remote(pb.at[4 * p + 2], fb.at[p], fs.at[p], fr.at[p], far_device)
-
-    def plain_copy(p):
-        return remote(pb.at[4 * p + plain_slot], nb.at[p, 0], ns.at[p, 0], nr.at[p, 0], plain_device)
-
-    def sum_copy(p):
-        return remote(pb.at[4 * p + near_slot], nb.at[p, 1], ns.at[p, 1], nr.at[p, 1], near_device)
-
-    for p in (1, 0):
-        far_copy(p).start()
-        plain_copy(p).start()
-
-    def relay(p):
-        far_copy(p).wait_recv()
-        total = pb[4 * p + near_slot].astype(F32) + fb[p].astype(F32)
-        pb[4 * p + near_slot] = total.astype(BF16)
-        sum_copy(p).start()
-
-    def collect(p):
-        plain_copy(p).wait_recv()
-        sum_copy(p).wait_recv()
-        return pb[4 * p].astype(F32) + nb[p, 0].astype(F32) + nb[p, 1].astype(F32)
-
-    mirror = remote(zs, zb, zsem, zr, me.group(0, 1))
-    relay(1)
-    zs[...] = collect(1).astype(BF16)
-    mirror.start()
+    block(0)
+    relay(1, 0)
+    relay(1, 1)
+    depart(0)
+    for h in range(2):
+        zs[:, part_of(h)] = collect(1, h).astype(BF16)
+        mirror_copy(h).start()
 
     shares = [
         remote(tfin, tall.at[me.x, half, c], bs.at[i], br.at[half, c], device)
@@ -621,7 +666,8 @@
             share.start()
         tall[me.x, half, c] = tfin[...]
 
-    relay(0)
+    relay(0, 0)
+    relay(0, 1)
     for b in range(2):
         for r in range(2):
             @pl.when(jnp.logical_not(jnp.logical_and(home, jnp.logical_and(half == b, c == r))))
@@ -635,10 +681,12 @@
     ]
     for copy in spreads:
         copy.start()
-    summed = collect(0)
-    mirror.wait_recv()
-    summed = summed + zb[...].astype(F32)
-    video_out[...] = (summed * mv[2:3].astype(F32)).astype(BF16)
+    for h in range(2):
+        summed = collect(0, h)
+        mirror_copy(h).wait_recv()
+        at = part_of(h)
+        summed = summed + zb[:, at].astype(F32)
+        video_out[:, at] = (summed * mv[2:3, at].astype(F32)).astype(BF16)
 
     for copy in spreads:
         copy.wait_recv()
@@ -647,11 +695,12 @@
             for r in range(2):
                 at = r * half_cols + k * (D // 8)
                 text_out[b * TXT : (b + 1) * TXT, at : at + D // 8] = tall[k, b, r]
-    for p in (0, 1):
-        far_copy(p).wait_send()
-        plain_copy(p).wait_send()
-        sum_copy(p).wait_send()
-    mirror.wait_send()
+    for h in range(2):
+        for p in (0, 1):
+            far_copy(p, h).wait_send()
+            plain_copy(p, h).wait_send()
+            sum_copy(p, h).wait_send()
+        mirror_copy(h).wait_send()
 
     @pl.when(jnp.logical_not(own_piece))
     def _():
@@ -688,7 +737,7 @@
             pltpu.VMEM((4, 2, 2, TXT, D // 8), BF16),
             pltpu.VMEM((2 * HD, D), BF16),
             pltpu.VMEM((2 * HD, half_cols), BF16),
-            DMA((2,)), DMA((2,)), DMA((2,)), DMA((2, 2)), DMA((2, 2)), DMA, DMA,
+            DMA((2,)), DMA((2, 2)), DMA((2, 2)), DMA((2, 2, 2)), DMA((2, 2, 2)), DMA((2,)), DMA((2,)),
             DMA((4,)), DMA((8,)), DMA((7,)), DMA((2, 2)), DMA((3,)), DMA((3,)),
         ],
         compiler_params=pltpu.CompilerParams(collective_id=1, has_side_effects=True),

time: 130 us -> 124 us (0.954)
  Pallas kernels: 125 us -> 119 us
    pallas_call x1, Pallas kernels: 42.4 us -> 33 us  [finish(): pl.pallas_call(finish_kernel, out_shape=(jax.ShapeDtypeStruct((CHUNK, D),...]
    pallas_call x1, Pallas kernels: 83.1 us -> 86.1 us  [mix(): pl.pallas_call(mix_kernel, out_shape=(jax.ShapeDtypeStruct((ROWS, 2 * HD)...]
where the time goes in v4:
time: 124 us; the launch traced here: 123 us
  Pallas kernels  119 us (96%)
  local copies, waits for them, and re-layouts  3.31 us (3%)
    pallas_call x1, Pallas kernels, mix(): pl.pallas_call(mix_kernel, out_shape=(jax.ShapeDtypeStruct((ROWS, 2 * HD)...  86.1 us
    pallas_call x1, Pallas kernels, finish(): pl.pallas_call(finish_kernel, out_shape=(jax.ShapeDtypeStruct((CHUNK, D),...  33 us
    unnamed x2, local copies, waits for them, and re-layouts  3.31 us

profile of v4, /device:TPU:1, one launch (start us, length us, event | category | flops | bytes accessed | tf_op | source)
XLA Modules:
  0.0 123.1 jit_solution(3542308084881838574)
XLA Ops:
  0.6 86.1 %mix.1 = (bf16[384,256]{1,0:T(8,128)(2,1)}, bf16[16,256]{1,0:T(8,128)(2,1)}) custom-call(bf16[48,3072]{1,0:T(8,128)(2,1)} %xv.1, bf16[32,3072]{1,0:T(8,128)(2,1)} %xt.1, bf16[3,3072]{1,0:T(4,128)(2,1)} %mv.3, bf16[3,3072]{1,0:T(4,128)(2,1)} %mt.3, f32[2,128]{1,0:T(2,128)} %gv.1, f32[2,128]{1,0:T(2,128)} %gt.1, bf16[3,3072,256]{2,1,0:T(8,128)(2,1)} %bitcast.2, ...), custom_call_target="tpu_custom_call" | custom-call | tf_op jit(solution)/shard_map/mix/pallas_call | solution.py:481
  86.7 33.0 %finish.1 = (bf16[48,3072]{1,0:T(8,128)(2,1)}, bf16[32,3072]{1,0:T(8,128)(2,1)}) custom-call(bf16[384,256]{1,0:T(8,128)(2,1)} %get-tuple-element.4.heads, bf16[16,256]{1,0:T(8,128)(2,1)} %get-tuple-element.5.theads, bf16[3,3072]{1,0:T(4,128)(2,1)} %mv.3, bf16[3,3072]{1,0:T(4,128)(2,1)} %mt.3, bf16[256,3072]{1,0:T(8,128)(2,1)} %wv_hbm.1, bf16[256,3072]{1,0:T(8,128)(2,1)} %wt_hbm.1), custom_call_target="tpu_custom_call" | custom-call | tf_op jit(solution)/shard_map/finish/pallas_call | solution.py:720
  119.7 1.7 %copy.14 = bf16[48,3072]{1,0:T(8,128)(2,1)} copy(bf16[48,3072]{1,0:T(8,128)(2,1)} %get-tuple-element.8) | data formatting | bytes 589824
  121.4 1.6 %copy.15 = bf16[32,3072]{1,0:T(8,128)(2,1)} copy(bf16[32,3072]{1,0:T(8,128)(2,1)} %get-tuple-element.9) | data formatting | bytes 393216

commit v5 on v4

--- a/solution.py
+++ b/solution.py
@@ -216,13 +216,13 @@
                 if d or i:
                     send(remote(
                         qkv.at[r, p, 0], q_rows(p, slot, c),
-                        qs.at[p, slot, i], qr.at[p, slot, i], along("x", d, r),
+                        qs.at[p, slot, i], qr.at[p, slot, i], along("zl", d, r),
                     ))
             for i, r in enumerate((c, other)):
                 if d or i:
                     send(remote(
                         qkv.at[r, p, pl.ds(1, 2)], kv_rows(p, slot, c),
-                        kvs.at[p, slot, i], kvr.at[p, slot, i], along("zl", d, r),
+                        kvs.at[p, slot, i], kvr.at[p, slot, i], along("x", d, r),
                     ))
 
     def exchange_text():
@@ -230,9 +230,9 @@
         pltpu.make_async_copy(tqkv.at[pl.ds(1, 2)], kv_text(0), tkr.at[0]).start()
         for d in (3, 1, 2):
             slot = (4 - d) % 4
-            send(remote(tqkv.at[0], q_text(slot), tqs.at[slot], tqr.at[slot], along("x", d, c)))
+            send(remote(tqkv.at[0], q_text(slot), tqs.at[slot], tqr.at[slot], along("zl", d, c)))
             send(remote(
-                tqkv.at[pl.ds(1, 2)], kv_text(slot), tks.at[slot], tkr.at[slot], along("zl", d, c)
+                tqkv.at[pl.ds(1, 2)], kv_text(slot), tks.at[slot], tkr.at[slot], along("x", d, c)
             ))
 
     def landed(dst, sem):
@@ -302,7 +302,7 @@
         lax.fori_loop(0, 2, pair, 0)
 
     def out_copies(p, j, slot, i, r):
-        device = along("x", j, r)
+        device = along("zl", j, r)
         return (
             remote(
                 ob.at[p, j, pl.ds(pl.multiple_of(r * HALF, HALF), HALF), :], orecv.at[p, slot, c],
@@ -375,7 +375,7 @@
                 if j == 0 and i == 0:
                     pltpu.make_async_copy(src, dst, tr.at[0, 0]).start()
                 else:
-                    send(remote(src, dst, ts.at[slot, i], tr.at[slot, i], along("x", j, r)))
+                    send(remote(src, dst, ts.at[slot, i], tr.at[slot, i], along("zl", j, r)))
 
     def merge_text():
         for slot in range(4):
@@ -424,11 +424,11 @@
         part = jnp.dot(trow[...], wt[j], preferred_element_type=F32)
         tqkv[j] = head_norm(part, gt[j : j + 1]) if j < 2 else part.astype(BF16)
     exchange_text()
-    await_kv(0)
-    open_phase(0)
     gathered(1)
     block(1)
     exchange(1)
+    await_kv(0)
+    open_phase(0)
     for j in range(4):
         landed(q_text(j), tqr.at[j])
     open_step(tq[...], tail)
@@ -745,6 +745,21 @@
     )(heads, theads, mv, mt, wv, wt)
 
 
+def settle_kernel(video, text, video_out, text_out):
+    video_out[...] = video[...]
+    text_out[...] = text[...]
+
+
+def settle(video, text):
+    return pl.pallas_call(
+        settle_kernel,
+        out_shape=tuple(jax.ShapeDtypeStruct(a.shape, a.dtype) for a in (video, text)),
+        in_specs=vmem(2),
+        out_specs=tuple(vmem(2)),
+        name="settle",
+    )(video, text)
+
+
 def local(
     video_tokens, text_tokens, video_modulation, text_modulation, video_projection,
     text_projection, video_output, text_output, video_gains, text_gains,
@@ -753,7 +768,9 @@
         video_tokens, text_tokens, video_modulation, text_modulation, video_gains, text_gains,
         jnp.transpose(video_projection, (1, 0, 2)), jnp.transpose(text_projection, (1, 0, 2)),
     )
-    return finish(heads, theads, video_modulation, text_modulation, video_output, text_output)
+    return settle(
+        *finish(heads, theads, video_modulation, text_modulation, video_output, text_output)
+    )
 
 
 def solution(mesh):

time: 124 us -> 112 us (0.903)
  Pallas kernels: 119 us -> 111 us
  local copies, waits for them, and re-layouts: 3.31 us -> 0 us
    pallas_call x1, Pallas kernels: 86.1 us -> 75.3 us  [mix(): pl.pallas_call(mix_kernel, out_shape=(jax.ShapeDtypeStruct((ROWS, 2 * HD)...]
    unnamed x2 -> x0, local copies, waits for them, and re-layouts: 3.31 us -> none
    pallas_call x0 -> x1, Pallas kernels: none -> 1.81 us  [settle(): pl.pallas_call(settle_kernel, out_shape=tuple((jax.ShapeDtypeStruct(a.sha...]
where the time goes in v5:
time: 112 us
  Pallas kernels  111 us (99%)
    pallas_call x1, Pallas kernels, mix(): pl.pallas_call(mix_kernel, out_shape=(jax.ShapeDtypeStruct((ROWS, 2 * HD)...  75.3 us
    pallas_call x1, Pallas kernels, finish(): pl.pallas_call(finish_kernel, out_shape=(jax.ShapeDtypeStruct((CHUNK, D),...  34.1 us

profile of v5, /device:TPU:1, one launch (start us, length us, event | category | flops | bytes accessed | tf_op | source)
XLA Modules:
  0.0 111.8 jit_solution(9836255946987607969)
XLA Ops:
  0.6 75.3 %mix.1 = (bf16[384,256]{1,0:T(8,128)(2,1)}, bf16[16,256]{1,0:T(8,128)(2,1)}) custom-call(bf16[48,3072]{1,0:T(8,128)(2,1)} %xv.1, bf16[32,3072]{1,0:T(8,128)(2,1)} %xt.1, bf16[3,3072]{1,0:T(4,128)(2,1)} %mv.3, bf16[3,3072]{1,0:T(4,128)(2,1)} %mt.3, f32[2,128]{1,0:T(2,128)} %gv.1, f32[2,128]{1,0:T(2,128)} %gt.1, bf16[3,3072,256]{2,1,0:T(8,128)(2,1)} %bitcast.2, ...), custom_call_target="tpu_custom_call" | custom-call | tf_op jit(solution)/shard_map/mix/pallas_call | solution.py:481
  75.9 34.1 %finish.1 = (bf16[48,3072]{1,0:T(8,128)(2,1)}, bf16[32,3072]{1,0:T(8,128)(2,1)}) custom-call(bf16[384,256]{1,0:T(8,128)(2,1)} %get-tuple-element.6.heads, bf16[16,256]{1,0:T(8,128)(2,1)} %get-tuple-element.7.theads, bf16[3,3072]{1,0:T(4,128)(2,1)} %mv.3, bf16[3,3072]{1,0:T(4,128)(2,1)} %mt.3, bf16[256,3072]{1,0:T(8,128)(2,1)} %wv_hbm.1, bf16[256,3072]{1,0:T(8,128)(2,1)} %wt_hbm.1), custom_call_target="tpu_custom_call" | custom-call | tf_op jit(solution)/shard_map/finish/pallas_call | solution.py:720
  110.0 1.8 %settle.1 = (bf16[48,3072]{1,0:T(8,128)(2,1)}, bf16[32,3072]{1,0:T(8,128)(2,1)}) custom-call(bf16[48,3072]{1,0:T(8,128)(2,1)} %get-tuple-element.8.video, bf16[32,3072]{1,0:T(8,128)(2,1)} %get-tuple-element.9.text), custom_call_target="tpu_custom_call" | custom-call | tf_op jit(solution)/shard_map/settle/pallas_call | solution.py:754

commit v6 on v5

--- a/solution.py
+++ b/solution.py
@@ -436,11 +436,11 @@
     await_kv(1)
     for j in range(4):
         landed(kv_text(j), tkr.at[j])
+    last_phase(1)
     send_text()
-    last_phase(1)
     last_phase(0)
+    merge(1)
     merge_text()
-    merge(1)
     merge(0)
 
     for pair in [mirror] + [found for move in moves for found in move]:
@@ -557,10 +557,6 @@
             def _():
                 pl.semaphore_signal(barrier, inc=1, device_id=giver(s), device_id_type=MESH)
 
-    load_t.wait()
-    part = jnp.dot(theads[...], wt[...], preferred_element_type=F32).astype(BF16)
-    for k in range(4):
-        tp[k] = part[:, k * (D // 8) : (k + 1) * (D // 8)]
     load_v.wait()
 
     def block(p):
@@ -625,6 +621,10 @@
         )
 
     depart(1)
+    load_t.wait()
+    part = jnp.dot(theads[...], wt[...], preferred_element_type=F32).astype(BF16)
+    for k in range(4):
+        tp[k] = part[:, k * (D // 8) : (k + 1) * (D // 8)]
     text_parts = [
         remote(tp.at[k], trb.at[mine], tss.at[k], trs.at[mine], gatherer(k)) for k in range(4)
     ]

time: 112 us -> 113 us (level)
  no operation moved by 1% of the time
where the time goes in v6:
time: 113 us
  Pallas kernels  112 us (99%)
    pallas_call x1, Pallas kernels, mix(): pl.pallas_call(mix_kernel, out_shape=(jax.ShapeDtypeStruct((ROWS, 2 * HD)...  75.9 us
    pallas_call x1, Pallas kernels, finish(): pl.pallas_call(finish_kernel, out_shape=(jax.ShapeDtypeStruct((CHUNK, D),...  34.6 us

profile of v6, /device:TPU:1, one launch (start us, length us, event | category | flops | bytes accessed | tf_op | source)
XLA Modules:
  0.0 113.0 jit_solution(6021535519257815449)
XLA Ops:
  0.6 75.9 %mix.1 = (bf16[384,256]{1,0:T(8,128)(2,1)}, bf16[16,256]{1,0:T(8,128)(2,1)}) custom-call(bf16[48,3072]{1,0:T(8,128)(2,1)} %xv.1, bf16[32,3072]{1,0:T(8,128)(2,1)} %xt.1, bf16[3,3072]{1,0:T(4,128)(2,1)} %mv.3, bf16[3,3072]{1,0:T(4,128)(2,1)} %mt.3, f32[2,128]{1,0:T(2,128)} %gv.1, f32[2,128]{1,0:T(2,128)} %gt.1, bf16[3,3072,256]{2,1,0:T(8,128)(2,1)} %bitcast.2, ...), custom_call_target="tpu_custom_call" | custom-call | tf_op jit(solution)/shard_map/mix/pallas_call | solution.py:481
  76.6 34.6 %finish.1 = (bf16[48,3072]{1,0:T(8,128)(2,1)}, bf16[32,3072]{1,0:T(8,128)(2,1)}) custom-call(bf16[384,256]{1,0:T(8,128)(2,1)} %get-tuple-element.6.heads, bf16[16,256]{1,0:T(8,128)(2,1)} %get-tuple-element.7.theads, bf16[3,3072]{1,0:T(4,128)(2,1)} %mv.3, bf16[3,3072]{1,0:T(4,128)(2,1)} %mt.3, bf16[256,3072]{1,0:T(8,128)(2,1)} %wv_hbm.1, bf16[256,3072]{1,0:T(8,128)(2,1)} %wt_hbm.1), custom_call_target="tpu_custom_call" | custom-call | tf_op jit(solution)/shard_map/finish/pallas_call | solution.py:720
  111.2 1.8 %settle.1 = (bf16[48,3072]{1,0:T(8,128)(2,1)}, bf16[32,3072]{1,0:T(8,128)(2,1)}) custom-call(bf16[48,3072]{1,0:T(8,128)(2,1)} %get-tuple-element.8.video, bf16[32,3072]{1,0:T(8,128)(2,1)} %get-tuple-element.9.text), custom_call_target="tpu_custom_call" | custom-call | tf_op jit(solution)/shard_map/settle/pallas_call | solution.py:754
